TPU v7x, 128 devices: a whole 4x4x4 slice. The times are simulated.
128 devices in a mesh: row: 16 (over x, z_hi, core), col: 8 (over z_lo, y).
Axes of the slice: x: 4, y: 4, z: 4 (z_hi: 2, z_lo: 2; z = z_hi * 2 + z_lo), core: 2. Of those that a mesh axis runs over, the one named last changes fastest.
Arguments:
- thin_line_values: float32 [2048, 65536], P('row', 'col'), may hold values from 0 to 65520, as said below
- occupied_patch_flags: int32 [16, 512], P('row', 'col'), may hold values 0 or 1
- leader_vertical_patch: int32 [2], replicated, may hold values from 0 to 511, as said below
- leader_square_lines: float32 [2, 128, 65536], P(None, 'row', 'col'), may hold values from 0 to 65520, as said below
- leader_square_reciprocals: float32 [2, 128, 128], replicated, may hold values from 0 to 65520, as said below
- remaining_destination_line: int32 [2048], P('row'), may hold values from 0 to 15, as said below
- leading_square_lines: float32 [512, 65536], P('row', 'col'), may hold values from 0 to 65520, as said below
- leading_square_reciprocal: float32 [512, 512], replicated, may hold values from 0 to 65520, as said below
Outputs:
- dense_grid: float32 [4096, 65536], P('row', 'col')
Inputs may be any that keep to these rules, and one draw needn't show every extreme that they name: `leader_vertical_patch`: distinct column tiles; the last column tile is among them. `remaining_destination_line`: among the rows of one index of row no value appears more than 16 times; one value, the same for every index of row, appears exactly 16 times in each. `thin_line_values`: Integers. `leader_square_lines`: Integers. `leader_square_reciprocals`: Integers. `leading_square_lines`: Integers. `leading_square_reciprocal`: Integers.
All inputs are finite; a program needn't handle non-finite values. No bound on the sum of `occupied_patch_flags` on one device may be relied on, other than what follows from the above.
Results may differ from a plain program's by a relative error of at most 0.0003.
Values sent between devices are 32-bit elements; how exact they have to be, the bound alone decides.
A program may use at most 256 MiB of HBM per device.

v0:
```python
import jax
import jax.numpy as jnp
from jax import lax
from jax.sharding import PartitionSpec as P

TILE = 128
PANEL = 512
NPIV = 2
MAX_PER_DEST = 16


modulus = 65521.0


def broadcast(block, axis, owner):
    block = jnp.where(lax.axis_index(axis) == owner, block, jnp.zeros_like(block))
    return lax.psum(block, axis)


def reduce_mod(values):
    quotient = jnp.floor(values / modulus)
    remain = values - quotient * modulus
    remain = jnp.where(remain < 0.0, remain + modulus, remain)
    return jnp.where(remain >= modulus, remain - modulus, remain)


def split_limbs(values):
    upper = jnp.floor(values / 256.0)
    return (upper.astype(jnp.bfloat16), (values - upper * 256.0).astype(jnp.bfloat16))


def mul_mod(left, right):
    left_hi, left_lo = split_limbs(left)
    right_hi, right_lo = split_limbs(right)
    total = jnp.zeros((left.shape[0], right.shape[1]), jnp.float32)
    for offset in range(0, left.shape[1], 128):
        a_hi = left_hi[:, offset : offset + 128]
        a_lo = left_lo[:, offset : offset + 128]
        b_hi = right_hi[offset : offset + 128]
        b_lo = right_lo[offset : offset + 128]
        high = jnp.dot(a_hi, b_hi, preferred_element_type=jnp.float32)
        cross = jnp.dot(a_hi, b_lo, preferred_element_type=jnp.float32) + jnp.dot(
            a_lo, b_hi, preferred_element_type=jnp.float32
        )
        low = jnp.dot(a_lo, b_lo, preferred_element_type=jnp.float32)
        part = reduce_mod(reduce_mod(cross) * 256.0) + reduce_mod(high) * 15.0 + reduce_mod(low)
        total = reduce_mod(total + part)
    return total


def share_multiplier(values, owner):
    return broadcast(values, "col", owner)


def dispatched_lines(chain_differential, remaining_destination_line):
    outbound_lines = lax.axis_size("row")
    indicator_matrix = (
        remaining_destination_line[:, None] == jnp.arange(outbound_lines, dtype=jnp.int32)[None, :]
    ).astype(jnp.int32)
    landing_order = jnp.sum((jnp.cumsum(indicator_matrix, axis=0) - 1) * indicator_matrix, axis=1)
    incoming_places = remaining_destination_line * MAX_PER_DEST + landing_order
    outgoing = (
        jnp.zeros((outbound_lines * MAX_PER_DEST, chain_differential.shape[1]), jnp.float32)
        .at[incoming_places]
        .set(chain_differential)
    )
    return lax.all_to_all(outgoing, "row", split_axis=0, concat_axis=0, tiled=True)


def panel_step(chain_differential, leading_square_lines, leading_square_reciprocal):
    panel_terms = mul_mod(chain_differential[:, :PANEL], leading_square_reciprocal)
    lower = broadcast(panel_terms, "col", 0)
    strip = lax.all_gather(leading_square_lines, "row", axis=0, tiled=True)
    update = mul_mod(lower, strip)
    return reduce_mod(chain_differential - update) / modulus


def local(
    thin_line_values,
    occupied_patch_flags,
    leader_vertical_patch,
    leader_square_lines,
    leader_square_reciprocals,
    remaining_destination_line,
    leading_square_lines,
    leading_square_reciprocal,
):
    rows_dev, width_dev = thin_line_values.shape
    tiles_dev = width_dev // TILE
    shaped = thin_line_values.reshape(rows_dev // TILE, TILE, tiles_dev, TILE)
    shaped = shaped * occupied_patch_flags.astype(jnp.float32)[:, None, :, None]
    eliminated_lines = shaped.reshape(rows_dev, width_dev)
    for pivot in range(NPIV):
        block_rows = lax.all_gather(leader_square_lines[pivot], "row", axis=0, tiled=True)
        column = leader_vertical_patch[pivot]
        owner = column // tiles_dev
        offset = column % tiles_dev * TILE
        tile_now, owner = (lax.dynamic_slice_in_dim(eliminated_lines, offset, TILE, 1), owner)
        factor = share_multiplier(mul_mod(tile_now, leader_square_reciprocals[pivot]), owner)
        eliminated_lines = reduce_mod(eliminated_lines - mul_mod(factor, block_rows))
    patchwise_arrangement = dispatched_lines(eliminated_lines, remaining_destination_line)
    return panel_step(patchwise_arrangement, leading_square_lines, leading_square_reciprocal)


def solution(mesh):
    return jax.shard_map(
        local,
        mesh=mesh,
        in_specs=(
            P("row", "col"),
            P("row", "col"),
            P(),
            P(None, "row", "col"),
            P(),
            P("row"),
            P("row", "col"),
            P(),
        ),
        out_specs=P("row", "col"),
        check_vma=False,
    )
```

profile of v0, /device:TPU:1, one launch (start us, length us, event | category | flops | bytes accessed | tf_op | source)
XLA Modules:
  0.0 635.3 jit_solution(7856029149557377119)
XLA Ops:
  7.4 1.4 fusion.224
  11.3 0.7 convert_bitcast_fusion
  12.1 2.6 broadcast_multiply_fusion
  15.0 1.7 copy-done.3
  16.9 1.7 fusion.121
  18.7 0.9 fusion.223
  19.7 0.5 all-gather.10.cloned.1.call-update
  23.2 66.9 %all-reduce.4.cloned.1.call-done = f32[128,128]{1,0:T(8,128)} async-done(((f32[128,128]{1,0:T(8,128)}), f32[128,128]{1,0:T(8,128)}) %all-reduce.4.cloned.1.call-update) | async-done | bytes 65552 | tf_op jit(solution)/shard_map/psum | solution.py:17
  90.1 3.3 fusion.167
  93.5 0.5 copy-done.1
  93.9 0.7 fusion.70
  94.7 0.8 fusion.169
  95.5 1.4 copy-done.4
  96.8 9.9 %compare_select_fusion.54 = f32[128,8192]{1,0:T(8,128)S(1)} fusion(f32[128,8192]{1,0:T(8,128)S(1)} %copy-done.4, f32[128,8192]{1,0:T(8,128)S(1)} %fusion.167, f32[128,8192]{1,0:T(8,128)S(1)} %fusion.70, f32[128,8192]{1,0:T(8,128)S(1)} %fusion.169, f32[1,128,8192]{2,1,0:T(8,128)S(1)} %copy-done.1, f32[128,128]{1,0:T(8,128)S(1)} %copy-done.7), kind=kOutput, calls=%fused_computation.58 | convolution fusion | flops 340869120 | bytes 25231360 | tf_op jit(solution)/shard_map/dot_general | solution.py:42
  107.2 1.6 copy-done.10
  108.7 0.9 fusion.125
  109.6 29.0 %all-gather.10.cloned.1.call-done = f32[1,128,8192]{2,1,0:T(8,128)} async-done(((f32[1,8,8192]{2,1,0:T(8,128)}), f32[1,128,8192]{2,1,0:T(8,128)}) %all-gather.10.cloned.1.call-update) | async-done | bytes 4194320 | tf_op jit(solution)/shard_map/all_gather | solution.py:94
  138.6 43.2 %all-reduce.6.cloned.1.call-done = f32[128,128]{1,0:T(8,128)} async-done(((f32[128,128]{1,0:T(8,128)}), f32[128,128]{1,0:T(8,128)}) %all-reduce.6.cloned.1.call-update) | async-done | bytes 65552 | tf_op jit(solution)/shard_map/psum | solution.py:17
  181.9 3.2 fusion.171
  185.0 0.3 copy-done
  185.3 0.7 fusion.67
  186.1 0.8 fusion.173
  186.9 1.4 copy-done.11
  188.2 9.4 %fusion.25 = f32[128,8192]{1,0:T(8,128)} fusion(f32[128,8192]{1,0:T(8,128)S(1)} %copy-done.11, f32[128,8192]{1,0:T(8,128)S(1)} %fusion.171, f32[128,8192]{1,0:T(8,128)S(1)} %fusion.67, f32[128,8192]{1,0:T(8,128)S(1)} %fusion.173, f32[1,128,8192]{2,1,0:T(8,128)S(1)} %copy-done, f32[128,128]{1,0:T(8,128)S(1)} %copy-done.8), kind=kOutput, calls=%fused_computation.100 | convolution fusion | flops 330383360 | bytes 25231360 | tf_op jit(solution)/shard_map/dot_general | solution.py:42
  197.6 9.7 %scatter_custom_fusion = f32[256,8192]{1,0:T(8,128)} fusion(s32[128]{0:T(128)S(1)} %compare_select_fusion.127, f32[128,8192]{1,0:T(8,128)} %fusion.25, f32[]{:T(128)} %constant.215.clone.1, f32[]{:T(128)} %constant.231.clone.1, f32[]{:T(128)} %constant.230.clone.1, f32[]{:T(128)} %constant.229.clone.1), kind=kCustom, calls=%fused_computation.101 | custom fusion | flops 10485760 | bytes 12585472 | tf_op jit(solution)/shard_map/scatter | solution.py:65
  207.4 12.2 %all-to-all-start = ((f32[16,16,8192]{2,1,0:T(8,128)}), f32[16,16,8192]{2,1,0:T(8,128)}, u32[]{:S(2)}, u32[]{:S(2)}) async-start(f32[16,16,8192]{2,1,0:T(8,128)} %bitcast.69), calls=%async_computation | async-start | bytes 16777216 | tf_op jit(solution)/shard_map/all_to_all | solution.py:67
  219.8 131.2 %all-to-all-done = f32[16,16,8192]{2,1,0:T(8,128)} async-done(((f32[16,16,8192]{2,1,0:T(8,128)}), f32[16,16,8192]{2,1,0:T(8,128)}, u32[]{:S(2)}, u32[]{:S(2)}) %all-to-all-start) | async-done | bytes 8388640 | tf_op jit(solution)/shard_map/all_to_all | solution.py:67
  351.0 1.1 subtract_convert_fusion.3
  352.4 0.2 fusion.107
  352.6 0.2 fusion.100
  352.8 0.2 fusion.111
  353.0 0.2 fusion.104
  353.2 0.2 fusion.97
  353.4 0.2 fusion.91
  353.6 0.2 fusion.95
  353.9 0.2 fusion.102
  354.1 0.2 fusion.109
  354.5 0.2 convolution_add_fusion.6
  354.7 0.2 convolution_add_fusion.7
  354.9 0.2 convolution_add_fusion.8
  355.1 0.2 convolution_add_fusion.9
  355.4 4.5 fusion.88
  360.0 0.5 all-gather.6.cloned.1.call-update
  360.5 71.4 %all-reduce.8.cloned.1.call-done = f32[256,512]{1,0:T(8,128)} async-done(((f32[256,512]{1,0:T(8,128)}), f32[256,512]{1,0:T(8,128)}) %all-reduce.8.cloned.1.call-update) | async-done | bytes 524304 | tf_op jit(solution)/shard_map/psum | solution.py:17
  431.9 1.1 subtract_convert_fusion.2
  433.0 48.9 %all-gather.6.cloned.1.call-done = f32[512,8192]{1,0:T(8,128)} async-done(((f32[32,8192]{1,0:T(8,128)}), f32[512,8192]{1,0:T(8,128)}) %all-gather.6.cloned.1.call-update) | async-done | bytes 16777232 | tf_op jit(solution)/shard_map/all_gather | solution.py:73
  481.9 7.8 %subtract_convert_fusion = (bf16[512,8192]{1,0:T(8,128)(2,1)S(1)}, bf16[512,8192]{1,0:T(8,128)(2,1)S(1)}) fusion(f32[512,8192]{1,0:T(8,128)} %all-gather.6.cloned.1.call-done), kind=kLoop, calls=%fused_computation.43 | loop fusion | flops 25165824 | bytes 33554432 | tf_op jit(solution)/shard_map/convert_element_type | solution.py:29
  489.7 4.5 fusion.62
  494.2 4.5 fusion.55
  498.7 4.5 fusion.48
  503.2 4.5 fusion.59
  507.6 4.5 fusion.52
  512.1 4.5 fusion.45
  516.6 4.6 fusion.39
  521.2 4.5 fusion.43
  525.7 4.5 fusion.50
  530.2 1.4 fusion.57
  531.7 1.2 fusion.64
  532.9 8.0 %convolution_add_fusion = f32[256,8192]{1,0:T(8,128)} fusion(f32[256,8192]{1,0:T(8,128)} %fusion.43, bf16[512,8192]{1,0:T(8,128)(2,1)S(1)} %get-tuple-element.6, bf16[256,512]{1,0:T(8,128)(2,1)S(1)} %get-tuple-element.11), kind=kOutput, calls=%fused_computation.70 | convolution fusion | flops 538968064 | bytes 18939904 | tf_op jit(solution)/shard_map/dot_general | solution.py:42
  540.9 8.1 %convolution_add_fusion.1 = f32[256,8192]{1,0:T(8,128)} fusion(f32[256,8192]{1,0:T(8,128)} %fusion.50, bf16[512,8192]{1,0:T(8,128)(2,1)S(1)} %get-tuple-element.6, bf16[256,512]{1,0:T(8,128)(2,1)S(1)} %get-tuple-element.11), kind=kOutput, calls=%fused_computation.71 | convolution fusion | flops 538968064 | bytes 18939904 | tf_op jit(solution)/shard_map/dot_general | solution.py:42
  549.0 4.5 convolution_add_fusion.2
  553.5 5.4 convolution_add_fusion.3
  558.9 0.8 copy-done.2
  559.7 68.0 %fusion.17 = f32[256,8192]{1,0:T(8,128)} fusion(f32[256,8192]{1,0:T(8,128)} %bitcast.9, f32[256,8192]{1,0:T(8,128)} %fusion.39, f32[256,8192]{1,0:T(8,128)} %convolution_add_fusion, f32[256,8192]{1,0:T(8,128)} %fusion.48, f32[256,8192]{1,0:T(8,128)} %fusion.45, f32[256,8192]{1,0:T(8,128)S(1)} %copy-done.2, f32[256,8192]{1,0:T(8,128)} %fusion.55, ...), kind=kOutput, calls=%fused_computation.92 | convolution fusion | flops 1021313024 | bytes 111214592 | tf_op jit(solution)/shard_map/dot_general | solution.py:45
  (44 shorter events, 2.2 us)
Async XLA Ops:
  7.4 82.8 %all-reduce.4.cloned.1.call-start = ((), (), s32[]{:S(2)}) async-start(), calls=%async_computation.1 | async-start | bytes 131072 | tf_op jit(solution)/shard_map/psum | solution.py:17
  12.1 2.7 copy-start.5
  12.1 6.6 %copy-start.9 = (f32[2,8,8192]{2,1,0:T(8,128)S(1)}, f32[2,8,8192]{2,1,0:T(8,128)}, u32[]{:S(2)}) copy-start(f32[2,8,8192]{2,1,0:T(8,128)} %param.11) | copy-start | bytes 1572868
  12.1 10.7 %copy-start.12 = (s32[128]{0:T(128)S(1)}, s32[128]{0:T(128)}, u32[]{:S(2)}) copy-start(s32[128]{0:T(128)} %param.13) | copy-start | bytes 1540
  14.7 2.0 copy-start.3
  18.6 71.5 %all-gather.8.cloned.1.call-start = ((), (), s32[]{:S(2)}) async-start(), calls=%async_computation.5 | async-start | bytes 4456448 | tf_op jit(solution)/shard_map/all_gather | solution.py:94
  19.6 119.0 %all-gather.10.cloned.1.call-start = ((), (), s32[]{:S(2)}) async-start(), calls=%async_computation.6 | async-start | bytes 4456448 | tf_op jit(solution)/shard_map/all_gather | solution.py:94
  20.2 161.7 %all-reduce.6.cloned.1.call-start = ((), (), s32[]{:S(2)}) async-start(), calls=%async_computation.2 | async-start | bytes 131072 | tf_op jit(solution)/shard_map/psum | solution.py:17
  90.1 3.3 copy-start.7
  90.1 3.8 copy-start.1
  94.6 2.2 copy-start.4
  106.7 2.0 copy-start.10
  181.9 3.5 copy-start
  181.9 3.5 copy-start.8
  186.1 2.2 copy-start.11
  207.3 12.2 %copy-start.6 = (f32[512,512]{1,0:T(8,128)S(1)}, f32[512,512]{1,0:T(8,128)}, u32[]{:S(2)}) copy-start(f32[512,512]{1,0:T(8,128)} %param.15) | copy-start | bytes 3145732
  207.4 143.7 %all-to-all-start = ((f32[16,16,8192]{2,1,0:T(8,128)}), f32[16,16,8192]{2,1,0:T(8,128)}, u32[]{:S(2)}, u32[]{:S(2)}) async-start(f32[16,16,8192]{2,1,0:T(8,128)} %bitcast.69), calls=%async_computation | async-start | bytes 16777216 | tf_op jit(solution)/shard_map/all_to_all | solution.py:67
  219.5 212.4 %all-reduce.8.cloned.1.call-start = ((), (), s32[]{:S(2)}) async-start(), calls=%async_computation.3 | async-start | bytes 1048576 | tf_op jit(solution)/shard_map/psum | solution.py:17
  359.9 122.0 %all-gather.6.cloned.1.call-start = ((), (), s32[]{:S(2)}) async-start(), calls=%async_computation.4 | async-start | bytes 17825792 | tf_op jit(solution)/shard_map/all_gather | solution.py:73
  553.5 6.2 copy-start.2
Sparse Core Ops, SparseCore 0:
  18.8 71.3 all-reduce.3
  109.8 72.0 all-reduce.5
  360.0 71.8 all-reduce.7
Sparse Core Ops, SparseCore 1:
  21.5 59.7 all-gather.7
  83.9 54.7 all-gather.9
  362.8 119.0 all-gather.5
where the time goes:
time: 645 us; the launch traced here: 635 us
  waiting for transfers between devices  392 us (61%)
  matrix products  177 us (27%)
  other arithmetic  23.7 us (4%)
  between operations  20.5 us (3%)
  starting transfers between devices  12.4 us (2%)
  local copies, waits for them, and re-layouts  9.99 us (2%)
    psum x3, waiting for transfers between devices, broadcast(): return lax.psum(block, axis)  182 us
    all_to_all x1, waiting for transfers between devices, dispatched_lines(): lax.all_to_all(outgoing, 'row', split_axis=0, concat_axis=0, tiled=True)  131 us
    dot_general x12, matrix products, mul_mod(): low = jnp.dot(a_lo, b_lo, preferred_element_type=jnp.float32)  93.4 us
    all_gather x1, waiting for transfers between devices, panel_step(): strip = lax.all_gather(leading_square_lines, 'row', axis=0, tiled=True)  48.9 us
    dot_general x12, matrix products, mul_mod(): jnp.dot(a_lo, b_hi, preferred_element_type=jnp.float32)  48.7 us
    all_gather x2, waiting for transfers between devices, local(): lax.all_gather(leader_square_lines[pivot], 'row', axis=0, tiled=True)  29 us
    dot_general x12, matrix products, mul_mod(): high = jnp.dot(a_hi, b_hi, preferred_element_type=jnp.float32)  20.6 us
    dot_general x12, matrix products, mul_mod(): jnp.dot(a_hi, b_lo, preferred_element_type=jnp.float32)  14.4 us
  transfers between devices with their start and end apart: 7, of which 6 were waited for; matrix products, arithmetic and copies ran while one was open for 3% of the time, Pallas kernels for 0%

commit v1 on v0

v1 whole, which is shorter than its diff:
```python
import functools

import jax
import jax.numpy as jnp
from jax import lax
from jax.experimental import pallas as pl
from jax.experimental.pallas import tpu as pltpu
from jax.sharding import PartitionSpec as P

TILE = 128
PANEL = 512
SLOTS = 16
MODULUS = 65521.0
INVERSE = 1.0 / 65521.0
MESH = pl.DeviceIdType.MESH
F32, BF16 = jnp.float32, jnp.bfloat16
ANY = pl.BlockSpec(memory_space=pl.ANY)
VM = pl.BlockSpec(memory_space=pltpu.VMEM)
SM = pl.BlockSpec(memory_space=pltpu.SMEM)


def dot(a, b):
    return jnp.dot(a, b, preferred_element_type=F32)


def nearest(values):
    return values - jnp.floor(values * INVERSE + 0.5) * MODULUS


def centred(values):
    return jnp.where(values > 32760.0, values - MODULUS, values)


def limbs(values):
    high = jnp.floor(values * (1.0 / 256.0) + 0.5)
    return high.astype(BF16), (values - high * 256.0).astype(BF16)


def subtract_product(base, left, right):
    (a_hi, a_lo), (b_hi, b_lo) = left, right
    cross = nearest(nearest(dot(a_hi, b_lo)) + dot(a_lo, b_hi))
    upper = nearest(256.0 * cross + 15.0 * nearest(dot(a_hi, b_hi)))
    return nearest(base - upper - dot(a_lo, b_lo))


def bucket_kernel(owned, flags, x_ref, dest_ref, piv_ref, out_ref, tile_ref, panel_ref, pick_ref):
    step = pl.program_id(0)
    block = x_ref.shape[1]
    tiles = block // TILE

    @pl.when(step == 0)
    def _():
        wide = jnp.broadcast_to(dest_ref[...], (TILE, TILE)).astype(F32)
        earlier = lax.broadcasted_iota(jnp.int32, (TILE, TILE), 0) < lax.broadcasted_iota(jnp.int32, (TILE, TILE), 1)
        same = jnp.where(earlier & (wide == wide.T), 1.0, 0.0)
        place = dest_ref[...].astype(F32) * SLOTS + jnp.sum(same, axis=0, keepdims=True)
        slot = lax.broadcasted_iota(jnp.int32, pick_ref.shape, 0).astype(F32)
        pick_ref[...] = jnp.where(slot == place, 1.0, 0.0).astype(BF16)
        tile_ref[...] = jnp.zeros_like(tile_ref)
        for t in range(PANEL // TILE):
            s = pl.ds(t * TILE, TILE)
            panel_ref[pl.ds(0, TILE), s] = x_ref[:, s] * flags[0, t].astype(F32)
        for k in range(2):
            panel_ref[pl.ds(TILE + 8 * k, 8), :] = piv_ref[k, :, :PANEL]

    pick = pick_ref[...]
    for t in range(tiles):
        s = pl.ds(t * TILE, TILE)
        x = x_ref[:, s] * flags[0, step * tiles + t].astype(F32)
        high = jnp.floor(x * (1.0 / 256.0))
        out_ref[:, s] = 256.0 * dot(pick, high.astype(BF16)) + dot(pick, (x - high * 256.0).astype(BF16))

    for k in range(2):
        tile = owned[k]

        @pl.when((tile >= step * tiles) & (tile < (step + 1) * tiles))
        def _():
            s = pl.ds(pl.multiple_of((tile - step * tiles) * TILE, TILE), TILE)
            tile_ref[pl.ds(0, TILE), pl.ds(k * TILE, TILE)] = x_ref[:, s] * flags[0, tile].astype(F32)
            if k == 1:
                tile_ref[pl.ds(TILE, 8), pl.ds(0, TILE)] = piv_ref[0, :, s]


def bucket(owned, flags, x, dest, piv):
    rows, width = x.shape
    block = 1024
    slots = 16 * SLOTS
    return pl.pallas_call(
        bucket_kernel,
        grid=(width // block,),
        in_specs=[
            SM,
            SM,
            pl.BlockSpec((rows, block), lambda i: (0, i)),
            pl.BlockSpec((1, rows), lambda i: (0, 0)),
            pl.BlockSpec((2, 8, block), lambda i: (0, 0, i)),
        ],
        out_specs=[
            pl.BlockSpec((slots, block), lambda i: (0, i)),
            pl.BlockSpec((rows + 8, 2 * TILE), lambda i: (0, 0)),
            pl.BlockSpec((rows + 16, PANEL), lambda i: (0, 0)),
            pl.BlockSpec((slots, rows), lambda i: (0, 0)),
        ],
        out_shape=[
            jax.ShapeDtypeStruct((slots, width), F32),
            jax.ShapeDtypeStruct((rows + 8, 2 * TILE), F32),
            jax.ShapeDtypeStruct((rows + 16, PANEL), F32),
            jax.ShapeDtypeStruct((slots, rows), BF16),
        ],
        name="bucket",
    )(owned, flags, x, dest, piv)


SENDS = [(1, 0, 0), (3, 0, 0), (0, 1, 0), (2, 0, 0), (1, 0, 1), (3, 0, 1), (0, 1, 1), (2, 0, 1),
         (1, 1, 0), (3, 1, 0), (2, 1, 0), (1, 1, 1), (3, 1, 1), (2, 1, 1), (0, 0, 1)]
NCHUNK = 4


def exchange_kernel(
    rows_ref, piv_ref, strip_ref, tile_ref, panel_ref, pick_ref,
    g_ref, ext_ref, pivs_ref, strips_ref, bx_ref,
    ext_out, bx_out, tile_in, panel_in,
    tile_s, tile_r, panel_s, panel_r, row_s, row_r, ext_s, ext_r, ag_s, ag_r, core_r, local_s,
):
    r, c = lax.axis_index("row"), lax.axis_index("col")
    x, h, core = r // 4, lax.rem(r // 2, 2), lax.rem(r, 2)

    def peer(dx, dh, dc):
        return lax.rem(x + dx, 4) * 4 + lax.rem(h + dh, 2) * 2 + lax.rem(core + dc, 2)

    def send(src, dst, ssem, rsem, row, col=c):
        return pltpu.make_async_remote_copy(
            src_ref=src, dst_ref=dst, send_sem=ssem, recv_sem=rsem, device_id=(row, col), device_id_type=MESH
        )

    barrier = pltpu.get_barrier_semaphore()
    for off in SENDS:
        pl.semaphore_signal(barrier, inc=1, device_id=(peer(*off), c), device_id_type=MESH)
    for k in range(1, 8):
        pl.semaphore_signal(barrier, inc=1, device_id=(r, lax.rem(c + k, 8)), device_id_type=MESH)
    pl.semaphore_wait(barrier, len(SENDS) + 7)

    tiles = [
        send(tile_ref, tile_in.at[k - 1], tile_s.at[k - 1], tile_r.at[k - 1], r, lax.rem(c + k, 8))
        for k in range(1, 8)
    ]
    panels = [
        send(panel_ref, panel_in, panel_s.at[k - 1], panel_r, r, k) for k in range(1, 8)
    ]
    for t in tiles:
        t.start()

    @pl.when(c == 0)
    def _():
        for p in panels:
            p.start()

    def slices(j, row):
        if j == 0:
            return piv_ref, pivs_ref.at[:, pl.ds(row * 8, 8)]
        if j == 3:
            return bx_out, bx_ref.at[row]
        half = strip_ref.shape[0] // 2
        return (
            strip_ref.at[pl.ds((j - 1) * half, half)],
            strips_ref.at[pl.ds(row * 2 * half + (j - 1) * half, half)],
        )

    RING = [(3, 0), (1, 0), (0, 1), (2, 0), (3, 1), (1, 1), (2, 1)]
    FROM_LEFT, FROM_RIGHT, FROM_PARTNER, FROM_FAR = 0, 1, 2, 3

    def own_copies(j):
        src, dst = slices(j, r)
        return [
            send(src, dst, ag_s.at[j, 0], ag_r.at[j, FROM_LEFT], peer(1, 0, 0)),
            send(src, dst, ag_s.at[j, 1], ag_r.at[j, FROM_RIGHT], peer(3, 0, 0)),
            send(src, dst, ag_s.at[j, 2], ag_r.at[j, FROM_PARTNER], peer(0, 1, 0)),
            send(src, dst, ag_s.at[j, 3], core_r.at[j, 7], peer(0, 0, 1)),
        ]

    def held(j, k):
        return slices(j, peer(RING[k][0], RING[k][1], 0))[1]

    def arrived(j, k):
        return send(held(j, k), held(j, k), ag_s.at[j, 0], ag_r.at[j, k], peer(0, 0, 1))

    def across(j, k):
        return send(held(j, k), held(j, k), ag_s.at[j, 8 + k], core_r.at[j, k], peer(0, 0, 1))

    def locals_(j):
        src, dst = slices(j, r)
        return pltpu.make_async_copy(src, dst, local_s.at[j])

    def onward_left(j):
        return send(held(j, 0), held(j, 0), ag_s.at[j, 4], ag_r.at[j, FROM_FAR], peer(1, 0, 0))

    def onward_right(j):
        return send(held(j, 1), held(j, 1), ag_s.at[j, 4], ag_r.at[j, FROM_FAR], peer(3, 0, 0))

    def partner_right(j):
        return send(held(j, 2), held(j, 2), ag_s.at[j, 5], ag_r.at[j, 4], peer(1, 0, 0))

    def partner_left(j):
        return send(held(j, 2), held(j, 2), ag_s.at[j, 6], ag_r.at[j, 5], peer(3, 0, 0))

    def far_across(j):
        return send(held(j, 3), held(j, 3), ag_s.at[j, 7], ag_r.at[j, 6], peer(0, 1, 0))

    def forward(j):
        odd = lax.rem(x + j, 2) == 1
        arrived(j, 0).wait_recv()
        pl.when(odd)(lambda: onward_left(j).start())
        across(j, 0).start()
        arrived(j, 1).wait_recv()
        pl.when(jnp.logical_not(odd))(lambda: onward_right(j).start())
        across(j, 1).start()
        arrived(j, 2).wait_recv()
        partner_right(j).start()
        partner_left(j).start()
        across(j, 2).start()
        arrived(j, 3).wait_recv()
        far_across(j).start()
        across(j, 3).start()

    for j in range(NCHUNK - 1):
        for copy in own_copies(j):
            copy.start()
        locals_(j).start()

    def row_copy(k):
        to = peer(*SENDS[k])
        return send(rows_ref.at[to], g_ref.at[r], row_s.at[k], row_r.at[k], to)

    own_rows = pltpu.make_async_copy(rows_ref.at[r], g_ref.at[r], local_s.at[NCHUNK])
    own_rows.start()
    for k in range(len(SENDS)):
        row_copy(k).start()

    total = tile_ref[...]
    for k in range(7):
        tiles[k].wait_recv()
        total = total + tile_in[k]

    @pl.when(c == 0)
    def _():
        panel_in[...] = panel_ref[...]

    @pl.when(c != 0)
    def _():
        panels[0].wait_recv()

    pick = pick_ref[...]
    for part, lo in ((total[:TILE, :], 0), (panel_in[pl.ds(0, TILE), :], 2 * TILE)):
        high = jnp.floor(part * (1.0 / 256.0))
        moved = 256.0 * dot(pick, high.astype(BF16)) + dot(pick, (part - high * 256.0).astype(BF16))
        ext_out[:, :, pl.ds(lo, part.shape[1])] = moved.reshape(16, SLOTS, part.shape[1])
    bx_out[...] = jnp.zeros_like(bx_out)
    bx_out[pl.ds(0, 8), pl.ds(0, TILE)] = total[TILE:, :TILE]
    bx_out[pl.ds(8, 16), :] = panel_in[pl.ds(TILE, 16), :]

    def ext_copy(k):
        to = peer(*SENDS[k])
        return send(ext_out.at[to], ext_ref.at[r], ext_s.at[k], ext_r.at[k], to)

    own_ext = pltpu.make_async_copy(ext_out.at[r], ext_ref.at[r], local_s.at[NCHUNK + 1])
    own_ext.start()
    for copy in own_copies(NCHUNK - 1):
        copy.start()
    locals_(NCHUNK - 1).start()
    for k in range(len(SENDS)):
        ext_copy(k).start()

    for j in range(NCHUNK):
        forward(j)
    for j in range(NCHUNK):
        for k in range(4, 7):
            arrived(j, k).wait_recv()
            across(j, k).start()

    def from_core(j, k):
        there = slices(j, peer(RING[k][0], RING[k][1], 1) if k < 7 else peer(0, 0, 1))[1]
        return send(there, there, ag_s.at[j, 0], core_r.at[j, k], peer(0, 0, 1))

    def row_in(k):
        dx, dh, dc = SENDS[k]
        return g_ref.at[peer(4 - dx, dh, dc)]

    def ext_in(k):
        dx, dh, dc = SENDS[k]
        return ext_ref.at[peer(4 - dx, dh, dc)]

    for j in range(NCHUNK):
        for k in range(8):
            from_core(j, k).wait_recv()
        for copy in own_copies(j):
            copy.wait_send()
        onward_left(j).wait_send()
        partner_right(j).wait_send()
        partner_left(j).wait_send()
        far_across(j).wait_send()
        for k in range(7):
            across(j, k).wait_send()
        locals_(j).wait()
    for k in range(len(SENDS)):
        send(row_in(k), row_in(k), row_s.at[k], row_r.at[k], peer(0, 0, 1)).wait_recv()
        row_copy(k).wait_send()
        send(ext_in(k), ext_in(k), ext_s.at[k], ext_r.at[k], peer(0, 0, 1)).wait_recv()
        ext_copy(k).wait_send()
    own_rows.wait()
    own_ext.wait()
    for t in tiles:
        t.wait_send()

    @pl.when(c == 0)
    def _():
        for p in panels:
            p.wait_send()


def exchange(rows, piv, strip, tile, panel, pick):
    width = rows.shape[2]
    dma = pltpu.SemaphoreType.DMA
    return pl.pallas_call(
        exchange_kernel,
        in_specs=[ANY, ANY, ANY, VM, VM, VM],
        out_specs=[ANY] * 5,
        out_shape=[
            jax.ShapeDtypeStruct((16, SLOTS, width), F32),
            jax.ShapeDtypeStruct((16, SLOTS, 2 * TILE + PANEL), F32),
            jax.ShapeDtypeStruct((2, TILE, width), F32),
            jax.ShapeDtypeStruct((PANEL, width), F32),
            jax.ShapeDtypeStruct((16, 24, PANEL), F32),
        ],
        scratch_shapes=[
            pltpu.VMEM((16, SLOTS, 2 * TILE + PANEL), F32),
            pltpu.VMEM((24, PANEL), F32),
            pltpu.VMEM((7,) + tile.shape, F32),
            pltpu.VMEM(panel.shape, F32),
            dma((7,)), dma((7,)), dma((7,)), dma(()),
            dma((15,)), dma((15,)), dma((15,)), dma((15,)),
            dma((NCHUNK, 15)), dma((NCHUNK, 7)), dma((NCHUNK, 8)), dma((NCHUNK + 2,)),
        ],
        name="exchange",
        compiler_params=pltpu.CompilerParams(collective_id=0, has_side_effects=True),
    )(rows, piv, strip, tile, panel, pick)


def eliminate_kernel(ext_ref, bx_ref, r_ref, big_ref, g_ref, piv_ref, strip_ref, out_ref, hi_ref, lo_ref):
    @pl.when(pl.program_id(0) == 0)
    def _():
        ext = ext_ref[...]
        bx = bx_ref[...]
        b0k1 = limbs(centred(bx[:, 0:8, :TILE].reshape(TILE, TILE)))
        b0p = limbs(centred(bx[:, 8:16, :].reshape(TILE, PANEL)))
        b1p = limbs(centred(bx[:, 16:24, :].reshape(TILE, PANEL)))
        zero = jnp.zeros((ext.shape[0], 1), F32)
        first = limbs(-subtract_product(zero, limbs(centred(ext[:, :TILE])), limbs(centred(r_ref[0]))))
        second = subtract_product(ext[:, TILE : 2 * TILE], first, b0k1)
        second = limbs(-subtract_product(zero, limbs(second), limbs(centred(r_ref[1]))))
        panel = subtract_product(ext[:, 2 * TILE :], first, b0p)
        panel = subtract_product(panel, second, b1p)
        lower = limbs(-subtract_product(zero, limbs(panel), limbs(centred(big_ref[...]))))
        for ref, i in ((hi_ref, 0), (lo_ref, 1)):
            ref[:, pl.ds(0, TILE)] = first[i]
            ref[:, pl.ds(TILE, TILE)] = second[i]
            ref[:, pl.ds(2 * TILE, PANEL)] = lower[i]

    rows = jnp.concatenate([piv_ref[0], piv_ref[1], strip_ref[...]], axis=0)
    result = subtract_product(g_ref[...], (hi_ref[...], lo_ref[...]), limbs(centred(rows)))
    out_ref[...] = jnp.where(result < 0.0, result + MODULUS, result) * INVERSE


def eliminate(ext, bx, recips, big, g, pivs, strips):
    slots, width = g.shape
    block = 512
    inner = 2 * TILE + PANEL
    whole = lambda a: pl.BlockSpec(a.shape, lambda i: (0,) * a.ndim)
    return pl.pallas_call(
        eliminate_kernel,
        grid=(width // block,),
        in_specs=[
            whole(ext), whole(bx), whole(recips), whole(big),
            pl.BlockSpec((slots, block), lambda i: (0, i)),
            pl.BlockSpec((2, TILE, block), lambda i: (0, 0, i)),
            pl.BlockSpec((PANEL, block), lambda i: (0, i)),
        ],
        out_specs=pl.BlockSpec((slots, block), lambda i: (0, i)),
        out_shape=jax.ShapeDtypeStruct((slots, width), F32),
        scratch_shapes=[pltpu.VMEM((slots, inner), BF16)] * 2,
        name="eliminate",
        compiler_params=pltpu.CompilerParams(vmem_limit_bytes=48 << 20),
    )(ext, bx, recips, big, g, pivs, strips)


def local(thin, flags, tiles, pivots, recips, dest, strip, big):
    width = thin.shape[1]
    owned = tiles - lax.axis_index("col") * (width // TILE)
    rows, tile, panel, pick = bucket(owned, flags, thin, dest[None, :], pivots)
    g, ext, pivs, strips, bx = exchange(rows.reshape(16, SLOTS, width), pivots, strip, tile, panel, pick)
    slots = 16 * SLOTS
    return eliminate(
        ext.reshape(slots, -1), bx, recips, big, g.reshape(slots, width), pivs, strips
    )


def solution(mesh):
    return jax.shard_map(
        local,
        mesh=mesh,
        in_specs=(
            P("row", "col"),
            P("row", "col"),
            P(),
            P(None, "row", "col"),
            P(),
            P("row"),
            P("row", "col"),
            P(),
        ),
        out_specs=P("row", "col"),
        check_vma=False,
    )
```

time: 645 us -> 270 us (0.42); the launches traced: 635 us -> 269 us
  waiting for transfers between devices: 392 us -> 0 us
  Pallas kernels: 0 us -> 265 us
  matrix products: 177 us -> 0 us
  other arithmetic: 23.7 us -> 1.26 us
  between operations: 20.5 us -> 0.04 us
  starting transfers between devices: 12.4 us -> 0 us
  local copies, waits for them, and re-layouts: 9.99 us -> 2.27 us
    pallas_call x0 -> x3, Pallas kernels: none -> 265 us  [the longest x1 225 us: exchange(): pl.pallas_call(exchange_kernel, in_specs=[ANY, ANY, ANY, VM, VM, VM], out...]
    psum x3 -> x0, waiting for transfers between devices: 182 us -> none  [broadcast(): return lax.psum(block, axis)]
    dot_general x48 -> x0, matrix products: 177 us -> none  [the longest x12 93.4 us: mul_mod(): low = jnp.dot(a_lo, b_lo, preferred_element_type=jnp.float32)]
    all_to_all x1 -> x0, waiting for transfers between devices: 131 us -> none  [dispatched_lines(): lax.all_to_all(outgoing, 'row', split_axis=0, concat_axis=0, tiled=True)]
    all_gather x3 -> x0, waiting for transfers between devices: 77.8 us -> none  [the longest x1 48.9 us: panel_step(): strip = lax.all_gather(leading_square_lines, 'row', axis=0, tiled=True)]
    all_to_all x1 -> x0, starting transfers between devices: 12.2 us -> none  [dispatched_lines(): lax.all_to_all(outgoing, 'row', split_axis=0, concat_axis=0, tiled=True)]
    convert_element_type x5 -> x0, other arithmetic: 10.3 us -> none  [the longest x4 10.3 us: split_limbs(): (values - upper * 256.0).astype(jnp.bfloat16)]
    scatter x1 -> x0, other arithmetic: 9.72 us -> none  [dispatched_lines(): outgoing = jnp.zeros((outbound_lines * MAX_PER_DEST, chain_differential.s...]
  transfers between devices with their start and end apart: 7 -> 0, of which waited for: 6 -> 0; matrix products, arithmetic and copies ran while one was open for 3% -> 0% of each run, Pallas kernels for 0% -> 0%
where the time goes in v1:
time: 270 us; the launch traced here: 269 us
  Pallas kernels  265 us (98%)
    pallas_call x1, Pallas kernels, exchange(): pl.pallas_call(exchange_kernel, in_specs=[ANY, ANY, ANY, VM, VM, VM], out...  225 us
    pallas_call x1, Pallas kernels, eliminate(): pl.pallas_call(eliminate_kernel, grid=(width // block,), in_specs=[whole(...  31.6 us
    pallas_call x1, Pallas kernels, bucket(): pl.pallas_call(bucket_kernel, grid=(width // block,), in_specs=[SM, SM, p...  9.11 us

profile of v1, /device:TPU:1, one launch (start us, length us, event | category | flops | bytes accessed | tf_op | source)
XLA Modules:
  0.0 268.9 jit_solution(13709862250228144105)
XLA Ops:
  0.0 0.0 copy-start
  0.0 0.0 copy-start.3
  0.0 1.3 broadcast_subtract_fusion.owned
  1.3 9.1 %bucket.1 = (f32[256,8192]{1,0:T(8,128)}, f32[136,256]{1,0:T(8,128)}, f32[144,512]{1,0:T(8,128)}, bf16[256,128]{1,0:T(8,128)(2,1)}) custom-call(s32[2]{0:T(128)} %broadcast_subtract_fusion.owned, s32[1,64]{1,0:T(1,128)} %flags.1, f32[128,8192]{1,0:T(8,128)} %x_ref.1, s32[1,128]{1,0:T(1,128)} %bitcast.7, f32[2,8,8192]{2,1,0:T(8,128)} %piv_ref.3), custom_call_target="tpu_custom_call" | custom-call | tf_op jit(solution)/shard_map/bucket/pallas_call | solution.py:88
  10.4 224.7 %exchange.1 = (f32[16,16,8192]{2,1,0:T(8,128)}, f32[16,16,768]{2,1,0:T(8,128)}, f32[2,128,8192]{2,1,0:T(8,128)}, f32[512,8192]{1,0:T(8,128)}, f32[16,24,512]{2,1,0:T(8,128)}) custom-call(f32[16,16,8192]{2,1,0:T(8,128)} %bitcast.5, f32[2,8,8192]{2,1,0:T(8,128)} %piv_ref.3, f32[32,8192]{1,0:T(8,128)} %strip_ref.1, f32[136,256]{1,0:T(8,128)} %get-tuple-element.15.tile_ref, ...), custom_call_target="tpu_custom_call" | custom-call | tf_op jit(solution)/shard_map/exchange/pallas_call | solution.py:323
  235.1 0.0 copy-done
  235.1 0.0 copy-done.3
  235.1 0.0 copy-start.1
  235.1 1.1 copy-done.1
  236.2 0.0 copy-start.2
  236.2 1.1 copy-done.2
  237.3 31.6 %eliminate.1 = f32[256,8192]{1,0:T(8,128)} custom-call(f32[256,768]{1,0:T(8,128)S(1)} %bitcast.4, f32[16,24,512]{2,1,0:T(8,128)S(1)} %copy-done.2, f32[2,128,128]{2,1,0:T(8,128)S(1)} %copy-done.3, f32[512,512]{1,0:T(8,128)S(1)} %copy-done, f32[256,8192]{1,0:T(8,128)} %bitcast.6, f32[2,128,8192]{2,1,0:T(8,128)} %get-tuple-element.21.piv_ref, ...), custom_call_target="tpu_custom_call" | custom-call | tf_op jit(solution)/shard_map/eliminate/pallas_call | solution.py:378
Async XLA Ops:
  0.0 235.1 %copy-start = (f32[512,512]{1,0:T(8,128)S(1)}, f32[512,512]{1,0:T(8,128)}, u32[]{:S(2)}) copy-start(f32[512,512]{1,0:T(8,128)} %big_ref.1) | copy-start | bytes 3145732
  0.0 235.1 %copy-start.3 = (f32[2,128,128]{2,1,0:T(8,128)S(1)}, f32[2,128,128]{2,1,0:T(8,128)}, u32[]{:S(2)}) copy-start(f32[2,128,128]{2,1,0:T(8,128)} %r_ref.1) | copy-start | bytes 393220
  235.1 1.1 copy-start.1
  236.2 1.1 copy-start.2

commit v2 on v1

v2 whole, which is shorter than its diff:
```python
import functools

import jax
import jax.numpy as jnp
from jax import lax
from jax.experimental import pallas as pl
from jax.experimental.pallas import tpu as pltpu
from jax.sharding import PartitionSpec as P

TILE = 128
PANEL = 512
SLOTS = 16
MODULUS = 65521.0
INVERSE = 1.0 / 65521.0
MESH = pl.DeviceIdType.MESH
F32, BF16 = jnp.float32, jnp.bfloat16
ANY = pl.BlockSpec(memory_space=pl.ANY)
VM = pl.BlockSpec(memory_space=pltpu.VMEM)
SM = pl.BlockSpec(memory_space=pltpu.SMEM)


def dot(a, b):
    return jnp.dot(a, b, preferred_element_type=F32)


def nearest(values):
    return values - jnp.floor(values * INVERSE + 0.5) * MODULUS


def centred(values):
    return jnp.where(values > 32760.0, values - MODULUS, values)


def limbs(values):
    high = jnp.floor(values * (1.0 / 256.0) + 0.5)
    return high.astype(BF16), (values - high * 256.0).astype(BF16)


def subtract_product(base, left, right):
    (a_hi, a_lo), (b_hi, b_lo) = left, right
    cross = nearest(nearest(dot(a_hi, b_lo)) + dot(a_lo, b_hi))
    upper = nearest(256.0 * cross + 15.0 * nearest(dot(a_hi, b_hi)))
    return nearest(base - upper - dot(a_lo, b_lo))


def bucket_kernel(owned, flags, x_ref, dest_ref, piv_ref, out_ref, tile_ref, panel_ref, pick_ref):
    step = pl.program_id(0)
    block = x_ref.shape[1]
    tiles = block // TILE

    @pl.when(step == 0)
    def _():
        wide = jnp.broadcast_to(dest_ref[...], (TILE, TILE)).astype(F32)
        earlier = lax.broadcasted_iota(jnp.int32, (TILE, TILE), 0) < lax.broadcasted_iota(jnp.int32, (TILE, TILE), 1)
        same = jnp.where(earlier & (wide == wide.T), 1.0, 0.0)
        place = dest_ref[...].astype(F32) * SLOTS + jnp.sum(same, axis=0, keepdims=True)
        slot = lax.broadcasted_iota(jnp.int32, pick_ref.shape, 0).astype(F32)
        pick_ref[...] = jnp.where(slot == place, 1.0, 0.0).astype(BF16)
        tile_ref[...] = jnp.zeros_like(tile_ref)
        for t in range(PANEL // TILE):
            s = pl.ds(t * TILE, TILE)
            panel_ref[pl.ds(0, TILE), s] = x_ref[:, s] * flags[0, t].astype(F32)
        for k in range(2):
            panel_ref[pl.ds(TILE + 8 * k, 8), :] = piv_ref[k, :, :PANEL]

    pick = pick_ref[...]
    for t in range(tiles):
        s = pl.ds(t * TILE, TILE)
        x = x_ref[:, s] * flags[0, step * tiles + t].astype(F32)
        high = jnp.floor(x * (1.0 / 256.0))
        out_ref[:, s] = 256.0 * dot(pick, high.astype(BF16)) + dot(pick, (x - high * 256.0).astype(BF16))

    for k in range(2):
        tile = owned[k]

        @pl.when((tile >= step * tiles) & (tile < (step + 1) * tiles))
        def _():
            s = pl.ds(pl.multiple_of((tile - step * tiles) * TILE, TILE), TILE)
            tile_ref[pl.ds(0, TILE), pl.ds(k * TILE, TILE)] = x_ref[:, s] * flags[0, tile].astype(F32)
            if k == 1:
                tile_ref[pl.ds(TILE, 8), pl.ds(0, TILE)] = piv_ref[0, :, s]


def bucket(owned, flags, x, dest, piv):
    rows, width = x.shape
    block = 1024
    slots = 16 * SLOTS
    return pl.pallas_call(
        bucket_kernel,
        grid=(width // block,),
        in_specs=[
            SM,
            SM,
            pl.BlockSpec((rows, block), lambda i: (0, i)),
            pl.BlockSpec((1, rows), lambda i: (0, 0)),
            pl.BlockSpec((2, 8, block), lambda i: (0, 0, i)),
        ],
        out_specs=[
            pl.BlockSpec((slots, block), lambda i: (0, i)),
            pl.BlockSpec((rows + 8, 2 * TILE), lambda i: (0, 0)),
            pl.BlockSpec((rows + 16, PANEL), lambda i: (0, 0)),
            pl.BlockSpec((slots, rows), lambda i: (0, 0)),
        ],
        out_shape=[
            jax.ShapeDtypeStruct((slots, width), F32),
            jax.ShapeDtypeStruct((rows + 8, 2 * TILE), F32),
            jax.ShapeDtypeStruct((rows + 16, PANEL), F32),
            jax.ShapeDtypeStruct((slots, rows), BF16),
        ],
        name="bucket",
    )(owned, flags, x, dest, piv)


OTHERS = [(1, 1, 0), (3, 0, 0), (3, 1, 0), (1, 0, 0), (2, 1, 0), (2, 0, 0), (0, 1, 0),
          (1, 1, 1), (3, 0, 1), (3, 1, 1), (1, 0, 1), (2, 1, 1), (2, 0, 1), (0, 1, 1), (0, 0, 1)]
SOURCES = [(3, 0), (1, 0), (0, 1), (2, 0), (3, 1), (1, 1), (2, 1)]
LEFT, RIGHT, PARTNER, FAR = 0, 1, 2, 3
GROUPS = 4
LINES = 48
BLOCK = 512
BX = GROUPS
EXT = 2 * TILE + PANEL


def exchange_kernel(
    rows_ref, piv_ref, strip_ref, tile_ref, panel_ref, pick_ref, r_ref, big_ref,
    out_ref,
    g, lines, ext, bx, ext_out, bx_out, tile_in, panel_in, hi_ref, lo_ref,
    tile_s, tile_r, panel_s, panel_r, row_s, row_r, ext_s, ext_r, ag_s, ag_r, core_r, local_s, out_s,
):
    r, c = lax.axis_index("row"), lax.axis_index("col")
    x, h, core = r // 4, lax.rem(r // 2, 2), lax.rem(r, 2)
    width = rows_ref.shape[2]
    span = width // GROUPS

    def peer(dx, dh, dc):
        return lax.rem(x + dx, 4) * 4 + lax.rem(h + dh, 2) * 2 + lax.rem(core + dc, 2)

    other = peer(0, 0, 1)

    def send(src, dst, ssem, rsem, row, col=c):
        return pltpu.make_async_remote_copy(
            src_ref=src, dst_ref=dst, send_sem=ssem, recv_sem=rsem, device_id=(row, col), device_id_type=MESH
        )

    def took(ref, sem):
        return pltpu.make_async_copy(ref, ref, sem).wait()

    barrier = pltpu.get_barrier_semaphore()
    for off in OTHERS:
        pl.semaphore_signal(barrier, inc=1, device_id=(peer(*off), c), device_id_type=MESH)
    for k in range(1, 8):
        pl.semaphore_signal(barrier, inc=1, device_id=(r, lax.rem(c + k, 8)), device_id_type=MESH)
    pl.semaphore_wait(barrier, len(OTHERS) + 7)

    tiles = [
        send(tile_ref, tile_in.at[k - 1], tile_s.at[k - 1], tile_r.at[k - 1], r, lax.rem(c + k, 8))
        for k in range(1, 8)
    ]
    panels = [send(panel_ref, panel_in, panel_s.at[k - 1], panel_r, r, k) for k in range(1, 8)]
    for t in tiles:
        t.start()

    @pl.when(c == 0)
    def _():
        for p in panels:
            p.start()

    def columns(j):
        return pl.ds(j * span, span)

    def slab(j, row):
        return bx.at[row] if j == BX else lines.at[row, :, columns(j)]

    def pieces(j):
        if j == BX:
            return [(bx_out, bx.at[r])]
        return [
            (piv_ref.at[:, columns(j)], lines.at[r, pl.ds(0, 16), columns(j)]),
            (strip_ref.at[:, columns(j)], lines.at[r, pl.ds(16, LINES - 16), columns(j)]),
        ]

    def own(j):
        for src, dst in pieces(j):
            send(src, dst, ag_s.at[j], ag_r.at[j, LEFT], peer(1, 0, 0)).start()
            send(src, dst, ag_s.at[j], ag_r.at[j, RIGHT], peer(3, 0, 0)).start()
            send(src, dst, ag_s.at[j], ag_r.at[j, PARTNER], peer(0, 1, 0)).start()
            send(src, dst, ag_s.at[j], core_r.at[j], other).start()
            pltpu.make_async_copy(src, dst, local_s.at[j]).start()

    def source(k):
        return peer(SOURCES[k][0], SOURCES[k][1], 0)

    def onward(j, k, rsem, row):
        held = slab(j, source(k))
        send(held, held, ag_s.at[j], rsem, row).start()

    def arrived(j, k):
        took(slab(j, source(k)), ag_r.at[j, k])

    def across(j, k):
        onward(j, k, core_r.at[j], other)

    def forward_near(j):
        odd = lax.rem(x + j, 2) == 1
        arrived(j, LEFT)
        pl.when(odd)(lambda: onward(j, LEFT, ag_r.at[j, FAR], peer(1, 0, 0)))
        across(j, LEFT)
        arrived(j, RIGHT)
        pl.when(jnp.logical_not(odd))(lambda: onward(j, RIGHT, ag_r.at[j, FAR], peer(3, 0, 0)))
        across(j, RIGHT)
        arrived(j, PARTNER)
        onward(j, PARTNER, ag_r.at[j, 4], peer(1, 0, 0))
        onward(j, PARTNER, ag_r.at[j, 5], peer(3, 0, 0))
        across(j, PARTNER)

    def forward_far(j):
        arrived(j, FAR)
        onward(j, FAR, ag_r.at[j, 6], peer(0, 1, 0))
        across(j, FAR)

    def forward_last(j):
        for k in (4, 5, 6):
            arrived(j, k)
            across(j, k)

    def rows_out(j):
        s = columns(j)
        for off in OTHERS:
            to = peer(*off)
            send(rows_ref.at[to, :, s], g.at[r, :, s], row_s.at[j], row_r.at[j], to).start()
        pltpu.make_async_copy(rows_ref.at[r, :, s], g.at[r, :, s], local_s.at[GROUPS + 1 + j]).start()

    def complete(j):
        s = columns(j)
        took(lines.at[pl.ds(0, 8), :, s], core_r.at[j])
        took(slab(j, r), local_s.at[j])
        took(g.at[pl.ds(0, 15), :, s], row_r.at[j])
        took(g.at[0, :, s], local_s.at[GROUPS + 1 + j])

    def compute(j):
        def block(i, _):
            s = pl.ds(pl.multiple_of(j * span + i * BLOCK, BLOCK), BLOCK)
            held = lines[:, :, s]
            rows = jnp.concatenate(
                [held[:, 0:8].reshape(TILE, BLOCK), held[:, 8:16].reshape(TILE, BLOCK),
                 held[:, 16:].reshape(PANEL, BLOCK)], axis=0
            )
            base = g[:, :, s].reshape(16 * SLOTS, BLOCK)
            result = subtract_product(base, (hi_ref[...], lo_ref[...]), limbs(centred(rows)))
            result = jnp.where(result < 0.0, result + MODULUS, result) * INVERSE
            g[:, :, s] = result.reshape(16, SLOTS, BLOCK)
            return 0

        lax.fori_loop(0, span // BLOCK, block, 0)
        pltpu.make_async_copy(g.at[:, :, columns(j)], out_ref.at[:, :, columns(j)], out_s.at[j]).start()

    def panel_columns():
        total = tile_ref[...]
        for k in range(7):
            tiles[k].wait_recv()
            total = total + tile_in[k]

        @pl.when(c == 0)
        def _():
            panel_in[...] = panel_ref[...]

        @pl.when(c != 0)
        def _():
            panels[0].wait_recv()

        pick = pick_ref[...]
        for part, at in ((total[:TILE, :], 0), (panel_in[pl.ds(0, TILE), :], 2 * TILE)):
            high = jnp.floor(part * (1.0 / 256.0))
            moved = 256.0 * dot(pick, high.astype(BF16)) + dot(pick, (part - high * 256.0).astype(BF16))
            ext_out[:, :, pl.ds(at, part.shape[1])] = moved.reshape(16, SLOTS, part.shape[1])
        bx_out[...] = jnp.zeros_like(bx_out)
        bx_out[pl.ds(0, 8), pl.ds(0, TILE)] = total[TILE:, :TILE]
        bx_out[pl.ds(8, 16), :] = panel_in[pl.ds(TILE, 16), :]
        own(BX)
        for off in OTHERS:
            to = peer(*off)
            send(ext_out.at[to], ext.at[r], ext_s, ext_r, to).start()
        pltpu.make_async_copy(ext_out.at[r], ext.at[r], local_s.at[2 * GROUPS + 1]).start()

    def multipliers():
        took(ext.at[pl.ds(0, 15)], ext_r)
        pltpu.make_async_copy(ext_out.at[r], ext.at[r], local_s.at[2 * GROUPS + 1]).wait()
        took(bx.at[pl.ds(0, 8)], core_r.at[BX])
        took(slab(BX, r), local_s.at[BX])
        terms = ext[...].reshape(16 * SLOTS, EXT)
        heads = bx[...]
        b0k1 = limbs(centred(heads[:, 0:8, :TILE].reshape(TILE, TILE)))
        b0p = limbs(centred(heads[:, 8:16, :].reshape(TILE, PANEL)))
        b1p = limbs(centred(heads[:, 16:24, :].reshape(TILE, PANEL)))
        zero = jnp.zeros((16 * SLOTS, 1), F32)
        first = limbs(-subtract_product(zero, limbs(centred(terms[:, :TILE])), limbs(centred(r_ref[0]))))
        second = subtract_product(terms[:, TILE : 2 * TILE], first, b0k1)
        second = limbs(-subtract_product(zero, limbs(second), limbs(centred(r_ref[1]))))
        panel = subtract_product(terms[:, 2 * TILE :], first, b0p)
        panel = subtract_product(panel, second, b1p)
        lower = limbs(-subtract_product(zero, limbs(panel), limbs(centred(big_ref[...]))))
        for ref, i in ((hi_ref, 0), (lo_ref, 1)):
            ref[:, pl.ds(0, TILE)] = first[i]
            ref[:, pl.ds(TILE, TILE)] = second[i]
            ref[:, pl.ds(2 * TILE, PANEL)] = lower[i]

    def begin(j):
        own(j)
        rows_out(j)

    begin(0)
    panel_columns()
    begin(1)
    forward_near(0)
    forward_near(BX)
    begin(2)
    forward_far(0)
    forward_near(1)
    forward_far(BX)
    begin(3)
    forward_last(0)
    forward_far(1)
    forward_near(2)
    forward_last(BX)
    forward_last(1)
    forward_far(2)
    forward_near(3)
    multipliers()
    forward_last(2)
    forward_far(3)
    complete(0)
    compute(0)
    forward_last(3)
    for j in range(1, GROUPS):
        complete(j)
        compute(j)

    for j in range(GROUPS + 1):
        whole = (bx if j == BX else lines.at[:, :, columns(j)])
        took(whole.at[pl.ds(0, 15)], ag_s.at[j])
    for j in range(GROUPS):
        took(g.at[pl.ds(0, 15), :, columns(j)], row_s.at[j])
        pltpu.make_async_copy(g.at[:, :, columns(j)], out_ref.at[:, :, columns(j)], out_s.at[j]).wait()
    took(ext.at[pl.ds(0, 15)], ext_s)
    for t in tiles:
        t.wait_send()

    @pl.when(c == 0)
    def _():
        for p in panels:
            p.wait_send()


def exchange(rows, piv, strip, tile, panel, pick, recips, big):
    width = rows.shape[2]
    dma = pltpu.SemaphoreType.DMA
    return pl.pallas_call(
        exchange_kernel,
        in_specs=[ANY, ANY, ANY, VM, VM, VM, VM, VM],
        out_specs=ANY,
        out_shape=jax.ShapeDtypeStruct((16, SLOTS, width), F32),
        scratch_shapes=[
            pltpu.VMEM((16, SLOTS, width), F32),
            pltpu.VMEM((16, LINES, width), F32),
            pltpu.VMEM((16, SLOTS, EXT), F32),
            pltpu.VMEM((16, 24, PANEL), F32),
            pltpu.VMEM((16, SLOTS, EXT), F32),
            pltpu.VMEM((24, PANEL), F32),
            pltpu.VMEM((7,) + tile.shape, F32),
            pltpu.VMEM(panel.shape, F32),
            pltpu.VMEM((16 * SLOTS, EXT), BF16),
            pltpu.VMEM((16 * SLOTS, EXT), BF16),
            dma((7,)), dma((7,)), dma((7,)), dma(()),
            dma((GROUPS,)), dma((GROUPS,)), dma(()), dma(()),
            dma((GROUPS + 1,)), dma((GROUPS + 1, 7)), dma((GROUPS + 1,)), dma((2 * GROUPS + 2,)), dma((GROUPS,)),
        ],
        name="exchange",
        compiler_params=pltpu.CompilerParams(
            collective_id=0, has_side_effects=True, vmem_limit_bytes=58 << 20
        ),
    )(rows, piv, strip, tile, panel, pick, recips, big)


def local(thin, flags, tiles, pivots, recips, dest, strip, big):
    width = thin.shape[1]
    owned = tiles - lax.axis_index("col") * (width // TILE)
    rows, tile, panel, pick = bucket(owned, flags, thin, dest[None, :], pivots)
    out = exchange(
        rows.reshape(16, SLOTS, width), pivots.reshape(16, width), strip, tile, panel, pick, recips, big
    )
    return out.reshape(16 * SLOTS, width)


def solution(mesh):
    return jax.shard_map(
        local,
        mesh=mesh,
        in_specs=(
            P("row", "col"),
            P("row", "col"),
            P(),
            P(None, "row", "col"),
            P(),
            P("row"),
            P("row", "col"),
            P(),
        ),
        out_specs=P("row", "col"),
        check_vma=False,
    )
```

time: 270 us -> 254 us (0.941)
  the two profiles are of different devices: /device:TPU:1 before, /device:TPU:114 now
where the time goes in v2:
time: 254 us; the launch traced here: 253 us
  Pallas kernels  245 us (96%)
  local copies, waits for them, and re-layouts  7.69 us (3%)
    pallas_call x1, Pallas kernels, exchange(): pl.pallas_call(exchange_kernel, in_specs=[ANY, ANY, ANY, VM, VM, VM, VM,...  235 us
    pallas_call x1, Pallas kernels, bucket(): pl.pallas_call(bucket_kernel, grid=(width // block,), in_specs=[SM, SM, p...  9.11 us
    unnamed x1, local copies, waits for them, and re-layouts  7.69 us

profile of v2, /device:TPU:114, one launch (start us, length us, event | category | flops | bytes accessed | tf_op | source)
XLA Modules:
  0.0 253.4 jit_solution(9788538105317590323)
XLA Ops:
  0.0 1.2 broadcast_subtract_fusion.owned
  1.2 9.1 %bucket.1 = (f32[256,8192]{1,0:T(8,128)}, f32[136,256]{1,0:T(8,128)}, f32[144,512]{1,0:T(8,128)}, bf16[256,128]{1,0:T(8,128)(2,1)}) custom-call(s32[2]{0:T(128)} %broadcast_subtract_fusion.owned, s32[1,64]{1,0:T(1,128)} %flags.1, f32[128,8192]{1,0:T(8,128)} %x_ref.1, s32[1,128]{1,0:T(1,128)} %bitcast.7, f32[2,8,8192]{2,1,0:T(8,128)} %piv_ref.1), custom_call_target="tpu_custom_call" | custom-call | tf_op jit(solution)/shard_map/bucket/pallas_call | solution.py:88
  10.3 235.4 %exchange.1 = f32[16,16,8192]{2,1,0:T(8,128)} custom-call(f32[16,16,8192]{2,1,0:T(8,128)} %bitcast.5, f32[16,8192]{1,0:T(8,128)} %bitcast.6, f32[32,8192]{1,0:T(8,128)} %strip_ref.1, f32[136,256]{1,0:T(8,128)} %get-tuple-element.10.tile_ref, f32[144,512]{1,0:T(8,128)} %get-tuple-element.11.panel_ref, bf16[256,128]{1,0:T(8,128)(2,1)} %get-tuple-element.12.pick_ref, ...), custom_call_target="tpu_custom_call" | custom-call | tf_op jit(solution)/shard_map/exchange/pallas_call | solution.py:358
  245.7 7.7 %copy.10 = f32[256,8192]{1,0:T(8,128)} copy(f32[256,8192]{1,0:T(8,128)} %bitcast.4) | data formatting | bytes 16777216

commit v3 on v0

v3 whole, which is shorter than its diff:
```python
import functools

import jax
import jax.numpy as jnp
from jax import lax
from jax.experimental import pallas as pl
from jax.experimental.pallas import tpu as pltpu
from jax.sharding import PartitionSpec as P

TILE = 128
PANEL = 512
SLOTS = 16
MODULUS = 65521.0
INVERSE = 1.0 / 65521.0
MESH = pl.DeviceIdType.MESH
F32, BF16 = jnp.float32, jnp.bfloat16
ANY = pl.BlockSpec(memory_space=pl.ANY)
VM = pl.BlockSpec(memory_space=pltpu.VMEM)
SM = pl.BlockSpec(memory_space=pltpu.SMEM)


def dot(a, b):
    return jnp.dot(a, b, preferred_element_type=F32)


def nearest(values):
    return values - jnp.floor(values * INVERSE + 0.5) * MODULUS


def centred(values):
    return jnp.where(values > 32760.0, values - MODULUS, values)


def limbs(values):
    high = jnp.floor(values * (1.0 / 256.0) + 0.5)
    return high.astype(BF16), (values - high * 256.0).astype(BF16)


def subtract_product(base, left, right):
    (a_hi, a_lo), (b_hi, b_lo) = left, right
    cross = nearest(nearest(dot(a_hi, b_lo)) + dot(a_lo, b_hi))
    upper = nearest(256.0 * cross + 15.0 * nearest(dot(a_hi, b_hi)))
    return nearest(base - upper - dot(a_lo, b_lo))


OTHERS = [(1, 1, 0), (3, 0, 0), (3, 1, 0), (1, 0, 0), (2, 1, 0), (2, 0, 0), (0, 1, 0),
          (1, 1, 1), (3, 0, 1), (3, 1, 1), (1, 0, 1), (2, 1, 1), (2, 0, 1), (0, 1, 1), (0, 0, 1)]
SOURCES = [(3, 0), (1, 0), (0, 1), (2, 0), (3, 1), (1, 1), (2, 1)]
LEFT, RIGHT, PARTNER, FAR = 0, 1, 2, 3
SPANS = [2048, 2048, 2048, 1024, 1024]
GROUPS = len(SPANS)
LINES = 48
BLOCK = 512
HEAD = SLOTS + 8


def exchange_kernel(
    owned, flags, dest_ref, thin_ref, piv_ref, strip_ref, r_hbm, big_hbm,
    g,
    lines, rows, thin, ext, ext_out, tile, tile_sum, tile_in, low, hi_ref, lo_ref, pick_ref, r_ref, big_ref,
    tile_s, tile_r, low_s, low_r, row_s, row_r, ext_s, ext_r, ag_s, ag_r, core_r, ag_l, row_l, ext_l, in_l, big_l,
):
    r, c = lax.axis_index("row"), lax.axis_index("col")
    x, h, core = r // 4, lax.rem(r // 2, 2), lax.rem(r, 2)
    plane, y = c // 4, lax.rem(c, 4)

    def columns(j):
        return pl.ds(sum(SPANS[:j]), SPANS[j])

    def thin_in(j):
        return pltpu.make_async_copy(thin_ref.at[:, columns(j)], thin.at[:, columns(j)], in_l.at[j])

    constants = [
        pltpu.make_async_copy(r_hbm, r_ref, big_l.at[0]),
        pltpu.make_async_copy(big_hbm, big_ref, big_l.at[1]),
    ]
    for j in range(GROUPS):
        thin_in(j).start()
    for copy in constants:
        copy.start()

    def peer(dx, dh, dc):
        return lax.rem(x + dx, 4) * 4 + lax.rem(h + dh, 2) * 2 + lax.rem(core + dc, 2)

    other = peer(0, 0, 1)
    across_z = lax.rem(c + 4, 8)

    def along_y(k):
        return plane * 4 + lax.rem(y + k, 4)

    def send(src, dst, ssem, rsem, row, col=c):
        return pltpu.make_async_remote_copy(
            src_ref=src, dst_ref=dst, send_sem=ssem, recv_sem=rsem, device_id=(row, col), device_id_type=MESH
        )

    def took(ref, sem):
        pltpu.make_async_copy(ref, ref, sem).wait()

    barrier = pltpu.get_barrier_semaphore()
    for off in OTHERS:
        pl.semaphore_signal(barrier, inc=1, device_id=(peer(*off), c), device_id_type=MESH)
    for col in (across_z, along_y(1), along_y(2), along_y(3)):
        pl.semaphore_signal(barrier, inc=1, device_id=(r, col), device_id_type=MESH)
    pl.semaphore_wait(barrier, len(OTHERS) + 4)

    def slab(j, row):
        return lines.at[row, :, columns(j)]

    def own(j):
        for src, dst in (
            (piv_ref.at[:, columns(j)], lines.at[r, pl.ds(0, 16), columns(j)]),
            (strip_ref.at[:, columns(j)], lines.at[r, pl.ds(16, LINES - 16), columns(j)]),
        ):
            send(src, dst, ag_s.at[j], ag_r.at[j, PARTNER], peer(0, 1, 0)).start()
            send(src, dst, ag_s.at[j], ag_r.at[j, LEFT], peer(1, 0, 0)).start()
            send(src, dst, ag_s.at[j], ag_r.at[j, RIGHT], peer(3, 0, 0)).start()
            send(src, dst, ag_s.at[j], core_r.at[j], other).start()
            pltpu.make_async_copy(src, dst, ag_l.at[j]).start()

    def source(k):
        return peer(SOURCES[k][0], SOURCES[k][1], 0)

    def onward(j, k, rsem, row):
        held = slab(j, source(k))
        send(held, held, ag_s.at[j], rsem, row).start()

    def arrived(j, k):
        took(slab(j, source(k)), ag_r.at[j, k])

    def across(j, k):
        onward(j, k, core_r.at[j], other)

    def near(j):
        odd = lax.rem(x + j, 2) == 1
        arrived(j, LEFT)
        pl.when(odd)(lambda: onward(j, LEFT, ag_r.at[j, FAR], peer(1, 0, 0)))
        across(j, LEFT)
        arrived(j, RIGHT)
        pl.when(jnp.logical_not(odd))(lambda: onward(j, RIGHT, ag_r.at[j, FAR], peer(3, 0, 0)))
        across(j, RIGHT)
        arrived(j, PARTNER)
        onward(j, PARTNER, ag_r.at[j, 4], peer(1, 0, 0))
        onward(j, PARTNER, ag_r.at[j, 5], peer(3, 0, 0))
        across(j, PARTNER)

    def far(j):
        arrived(j, FAR)
        onward(j, FAR, ag_r.at[j, 6], peer(0, 1, 0))
        across(j, FAR)

    def last(j):
        for k in (4, 5, 6):
            arrived(j, k)
            across(j, k)

    def choose():
        wide = jnp.broadcast_to(dest_ref[...], (TILE, TILE)).astype(F32)
        earlier = lax.broadcasted_iota(jnp.int32, (TILE, TILE), 0) < lax.broadcasted_iota(jnp.int32, (TILE, TILE), 1)
        same = jnp.where(earlier & (wide == wide.T), 1.0, 0.0)
        place = dest_ref[...].astype(F32) * SLOTS + jnp.sum(same, axis=0, keepdims=True)
        slot = lax.broadcasted_iota(jnp.int32, pick_ref.shape, 0).astype(F32)
        pick_ref[...] = jnp.where(slot == place, 1.0, 0.0).astype(BF16)

    def picked(part):
        high = jnp.floor(part * (1.0 / 256.0))
        moved = 256.0 * dot(pick_ref[...], high.astype(BF16)) + dot(pick_ref[...], (part - high * 256.0).astype(BF16))
        return moved.reshape(16, SLOTS, part.shape[1])

    def flag(t):
        return flags[0, t].astype(F32)

    def fill(j):
        start = sum(SPANS[:j])

        def block(i, _):
            s = pl.ds(pl.multiple_of(start + i * BLOCK, BLOCK), BLOCK)
            first = start // TILE + i * (BLOCK // TILE)
            mask = jnp.concatenate([jnp.full((1, TILE), flag(first + t), F32) for t in range(BLOCK // TILE)], axis=1)
            part = thin[:, s] * mask
            rows[:, :, s] = picked(part)
            for t in range(BLOCK // TILE):
                for k in range(2):
                    chosen = jnp.where(owned[k] == first + t, 1.0, 0.0)
                    into = pl.ds(0, TILE), pl.ds(k * TILE, TILE)
                    tile[into] += part[:, t * TILE : (t + 1) * TILE] * chosen
                at = pl.multiple_of(start + i * BLOCK + t * TILE, TILE)
                tile[pl.ds(TILE, 8), pl.ds(0, TILE)] += piv_ref[pl.ds(0, 8), pl.ds(at, TILE)] * chosen
            return 0

        lax.fori_loop(0, SPANS[j] // BLOCK, block, 0)

    def rows_out(j):
        s = columns(j)
        for off in OTHERS:
            to = peer(*off)
            send(rows.at[to, :, s], g.at[r, :, s], row_s.at[j], row_r.at[j], to).start()
        pltpu.make_async_copy(rows.at[r, :, s], g.at[r, :, s], row_l.at[j]).start()

    def tile_across():
        return send(tile, tile_in.at[0], tile_s.at[0], tile_r.at[0], r, across_z)

    def tile_along(k):
        return send(tile_sum, tile_in.at[k], tile_s.at[k], tile_r.at[k], r, along_y(k))

    def tile_next():
        tile_across().wait_recv()
        tile_sum[...] = tile[...] + tile_in[0]
        for k in (1, 2, 3):
            tile_along(k).start()

    def ext_begin():
        total = tile_sum[...]
        for k in (1, 2, 3):
            tile_along(k).wait_recv()
            total = total + tile_in[k]
        ext_out[:, pl.ds(0, SLOTS), :] = picked(total[:TILE, :])
        ext_out[:, pl.ds(SLOTS, 8), :] = jnp.broadcast_to(total[TILE:, :][None], (16, 8, 2 * TILE))
        for off in OTHERS:
            to = peer(*off)
            send(ext_out.at[to], ext.at[r], ext_s, ext_r, to).start()
        pltpu.make_async_copy(ext_out.at[r], ext.at[r], ext_l).start()

    def keep(parts, at):
        for ref, part in zip((hi_ref, lo_ref), parts):
            ref[:, pl.ds(at, part.shape[1])] = part

    def kept(at):
        return hi_ref[:, pl.ds(at, TILE)], lo_ref[:, pl.ds(at, TILE)]

    zero = jnp.zeros((16 * SLOTS, 1), F32)

    def factors():
        took(ext.at[pl.ds(0, 15)], ext_r)
        took(ext.at[0], ext_l)
        for copy in constants:
            copy.wait()
        terms = ext[:, :SLOTS, :].reshape(16 * SLOTS, 2 * TILE)
        pivot = limbs(centred(ext[:, SLOTS:, :TILE].reshape(TILE, TILE)))
        first = limbs(-subtract_product(zero, limbs(centred(terms[:, :TILE])), limbs(centred(r_ref[0]))))
        second = subtract_product(terms[:, TILE:], first, pivot)
        second = limbs(-subtract_product(zero, limbs(second), limbs(centred(r_ref[1]))))
        keep(first, 0)
        keep(second, TILE)

    def low_out(k):
        col = (1, 2, 3, 4)[k]
        return send(low, low, low_s.at[k], low_r, r, col)

    def low_next(k):
        return send(low, low, low_s.at[k], low_r, r, 5 + k)

    def lower_begin():
        @pl.when(c == 0)
        def _():
            base = g[:, :, :PANEL].reshape(16 * SLOTS, PANEL)
            for k in range(2):
                part = lines[:, 8 * k : 8 * k + 8, :PANEL].reshape(TILE, PANEL)
                base = subtract_product(base, kept(k * TILE), limbs(centred(part)))
            low[...] = -subtract_product(zero, limbs(base), limbs(centred(big_ref[...])))
            for k in (3, 0, 1, 2):
                low_out(k).start()

        @pl.when(c == 4)
        def _():
            low_out(3).wait_recv()
            for k in range(3):
                low_next(k).start()

    def lower_end():
        @pl.when((c != 0) & (c != 4))
        def _():
            low_out(3).wait_recv()

        keep(limbs(low[...]), 2 * TILE)

    def complete(j):
        s = columns(j)
        took(lines.at[pl.ds(0, 8), :, s], core_r.at[j])
        took(slab(j, r), ag_l.at[j])
        took(g.at[pl.ds(0, 15), :, s], row_r.at[j])
        took(g.at[0, :, s], row_l.at[j])

    def compute(j):
        start = sum(SPANS[:j])

        def block(i, _):
            s = pl.ds(pl.multiple_of(start + i * BLOCK, BLOCK), BLOCK)
            held = lines[:, :, s]
            inner = jnp.concatenate(
                [held[:, 0:8].reshape(TILE, BLOCK), held[:, 8:16].reshape(TILE, BLOCK),
                 held[:, 16:].reshape(PANEL, BLOCK)], axis=0
            )
            base = g[:, :, s].reshape(16 * SLOTS, BLOCK)
            result = subtract_product(base, (hi_ref[...], lo_ref[...]), limbs(centred(inner)))
            result = jnp.where(result < 0.0, result + MODULUS, result) * INVERSE
            g[:, :, s] = result.reshape(16, SLOTS, BLOCK)
            return 0

        lax.fori_loop(0, SPANS[j] // BLOCK, block, 0)

    for j in range(GROUPS):
        own(j)
    choose()
    tile[...] = jnp.zeros_like(tile)
    for j in range(GROUPS):
        thin_in(j).wait()
    fill(0)
    rows_out(0)
    for j in range(1, GROUPS):
        fill(j)
    tile_across().start()
    near(0)
    near(1)
    rows_out(1)
    tile_next()
    near(2)
    far(0)
    ext_begin()
    near(3)
    far(1)
    near(4)
    rows_out(2)
    far(2)
    last(0)
    far(3)
    last(1)
    rows_out(3)
    factors()
    far(4)
    last(2)
    rows_out(4)
    complete(0)
    lower_begin()
    last(3)
    last(4)
    lower_end()
    compute(0)
    for j in range(1, GROUPS):
        complete(j)
        compute(j)

    for j in range(GROUPS):
        took(lines.at[pl.ds(0, 15), :, columns(j)], ag_s.at[j])
        took(g.at[pl.ds(0, 15), :, columns(j)], row_s.at[j])
    took(ext.at[pl.ds(0, 15)], ext_s)
    tile_across().wait_send()
    for k in (1, 2, 3):
        tile_along(k).wait_send()

    @pl.when(c == 0)
    def _():
        for k in range(4):
            low_out(k).wait_send()

    @pl.when(c == 4)
    def _():
        for k in range(3):
            low_next(k).wait_send()


def exchange(owned, flags, dest, thin, piv, strip, recips, big):
    width = thin.shape[1]
    dma = pltpu.SemaphoreType.DMA
    head = (TILE + 8, 2 * TILE)
    return pl.pallas_call(
        exchange_kernel,
        in_specs=[SM, SM, VM, ANY, VM, ANY, ANY, ANY],
        out_specs=VM,
        out_shape=pltpu.VMEM((16, SLOTS, width), F32),
        scratch_shapes=[
            pltpu.VMEM((16, LINES, width), F32),
            pltpu.VMEM((16, SLOTS, width), F32),
            pltpu.VMEM(thin.shape, F32),
            pltpu.VMEM((16, HEAD, 2 * TILE), F32),
            pltpu.VMEM((16, HEAD, 2 * TILE), F32),
            pltpu.VMEM(head, F32),
            pltpu.VMEM(head, F32),
            pltpu.VMEM((4,) + head, F32),
            pltpu.VMEM((16 * SLOTS, PANEL), F32),
            pltpu.VMEM((16 * SLOTS, 2 * TILE + PANEL), BF16),
            pltpu.VMEM((16 * SLOTS, 2 * TILE + PANEL), BF16),
            pltpu.VMEM((16 * SLOTS, TILE), BF16),
            pltpu.VMEM(recips.shape, F32),
            pltpu.VMEM(big.shape, F32),
            dma((4,)), dma((4,)), dma((4,)), dma(()),
            dma((GROUPS,)), dma((GROUPS,)), dma(()), dma(()),
            dma((GROUPS,)), dma((GROUPS, 7)), dma((GROUPS,)),
            dma((GROUPS,)), dma((GROUPS,)), dma(()), dma((GROUPS,)), dma((2,)),
        ],
        name="exchange",
        compiler_params=pltpu.CompilerParams(
            collective_id=0, has_side_effects=True, vmem_limit_bytes=52 << 20
        ),
    )(owned, flags, dest, thin, piv, strip, recips, big)


def local(thin, flags, tiles, pivots, recips, dest, strip, big):
    width = thin.shape[1]
    owned = tiles - lax.axis_index("col") * (width // TILE)
    out = exchange(owned, flags, dest[None, :], thin, pivots.reshape(16, width), strip, recips, big)
    return out.reshape(16 * SLOTS, width)


def solution(mesh):
    return jax.shard_map(
        local,
        mesh=mesh,
        in_specs=(
            P("row", "col"),
            P("row", "col"),
            P(),
            P(None, "row", "col"),
            P(),
            P("row"),
            P("row", "col"),
            P(),
        ),
        out_specs=P("row", "col"),
        check_vma=False,
    )
```

time: 645 us -> 246 us (0.38)
  the two profiles are of different devices: /device:TPU:1 before, /device:TPU:48 now
where the time goes in v3:
time: 246 us
  Pallas kernels  242 us (98%)
  local copies, waits for them, and re-layouts  3.4 us (1%)
    pallas_call x1, Pallas kernels, exchange(): pl.pallas_call(exchange_kernel, in_specs=[SM, SM, VM, ANY, VM, ANY, ANY,...  242 us

profile of v3, /device:TPU:48, one launch (start us, length us, event | category | flops | bytes accessed | tf_op | source)
XLA Modules:
  0.0 246.2 jit_solution(7310169176159515075)
XLA Ops:
  0.0 1.2 broadcast_subtract_fusion.owned
  1.2 241.6 %exchange.1 = f32[16,16,8192]{2,1,0:T(8,128)S(1)} custom-call(s32[2]{0:T(128)} %broadcast_subtract_fusion.owned, s32[1,64]{1,0:T(1,128)} %flags.1, s32[1,128]{1,0:T(1,128)} %bitcast.5, f32[128,8192]{1,0:T(8,128)} %thin_ref.1, f32[16,8192]{1,0:T(8,128)} %bitcast.4, f32[32,8192]{1,0:T(8,128)} %strip_ref.1, f32[2,128,128]{2,1,0:T(8,128)} %r_hbm.1, ...), custom_call_target="tpu_custom_call" | custom-call | tf_op jit(solution)/shard_map/exchange/pallas_call | solution.py:365
  242.8 3.4 %copy.10 = f32[256,8192]{1,0:T(8,128)} copy(f32[256,8192]{1,0:T(8,128)S(1)} %bitcast.3) | data formatting | bytes 16777216

commit v4 on v3

--- a/solution.py
+++ b/solution.py
@@ -47,7 +47,7 @@
           (1, 1, 1), (3, 0, 1), (3, 1, 1), (1, 0, 1), (2, 1, 1), (2, 0, 1), (0, 1, 1), (0, 0, 1)]
 SOURCES = [(3, 0), (1, 0), (0, 1), (2, 0), (3, 1), (1, 1), (2, 1)]
 LEFT, RIGHT, PARTNER, FAR = 0, 1, 2, 3
-SPANS = [2048, 2048, 2048, 1024, 1024]
+SPANS = [512, 2560, 2048, 1536, 1024, 512]
 GROUPS = len(SPANS)
 LINES = 48
 BLOCK = 512
@@ -298,46 +298,64 @@
 
         lax.fori_loop(0, SPANS[j] // BLOCK, block, 0)
 
-    for j in range(GROUPS):
-        own(j)
+    own(0)
+    own(1)
     choose()
     tile[...] = jnp.zeros_like(tile)
     for j in range(GROUPS):
         thin_in(j).wait()
     fill(0)
     rows_out(0)
-    for j in range(1, GROUPS):
-        fill(j)
+    near(0)
+    fill(1)
+    fill(2)
+    far(0)
+    fill(3)
+    fill(4)
+    fill(5)
     tile_across().start()
-    near(0)
+    last(0)
+    own(2)
+    own(3)
     near(1)
+    tile_next()
+    own(4)
+    own(5)
+    ext_begin()
+    near(2)
     rows_out(1)
-    tile_next()
-    near(2)
-    far(0)
-    ext_begin()
+    far(1)
     near(3)
-    far(1)
-    near(4)
-    rows_out(2)
-    far(2)
-    last(0)
-    far(3)
-    last(1)
-    rows_out(3)
     factors()
-    far(4)
-    last(2)
-    rows_out(4)
     complete(0)
     lower_begin()
-    last(3)
-    last(4)
+    near(4)
+    near(5)
+    far(2)
+    rows_out(2)
+    last(1)
+    far(3)
+    last(2)
+    rows_out(3)
+    far(4)
+    far(5)
+    rows_out(4)
+    rows_out(5)
     lower_end()
     compute(0)
-    for j in range(1, GROUPS):
-        complete(j)
-        compute(j)
+    last(3)
+    complete(1)
+    compute(1)
+    last(4)
+    complete(2)
+    compute(2)
+    last(5)
+    complete(3)
+    compute(3)
+    complete(4)
+    compute(4)
+    complete(5)
+    compute(5)
 
     for j in range(GROUPS):
         took(lines.at[pl.ds(0, 15), :, columns(j)], ag_s.at[j])

time: 246 us -> 211 us (0.86)
  the two profiles are of different devices: /device:TPU:48 before, /device:TPU:1 now
where the time goes in v4:
time: 211 us; the launch traced here: 210 us
  Pallas kernels  206 us (98%)
  local copies, waits for them, and re-layouts  3.4 us (2%)
    pallas_call x1, Pallas kernels, exchange(): pl.pallas_call(exchange_kernel, in_specs=[SM, SM, VM, ANY, VM, ANY, ANY,...  206 us

profile of v4, /device:TPU:1, one launch (start us, length us, event | category | flops | bytes accessed | tf_op | source)
XLA Modules:
  0.0 210.2 jit_solution(16534562057053011916)
XLA Ops:
  0.0 1.2 broadcast_subtract_fusion.owned
  1.2 205.7 %exchange.1 = f32[16,16,8192]{2,1,0:T(8,128)S(1)} custom-call(s32[2]{0:T(128)} %broadcast_subtract_fusion.owned, s32[1,64]{1,0:T(1,128)} %flags.1, s32[1,128]{1,0:T(1,128)} %bitcast.5, f32[128,8192]{1,0:T(8,128)} %thin_ref.1, f32[16,8192]{1,0:T(8,128)} %bitcast.4, f32[32,8192]{1,0:T(8,128)} %strip_ref.1, f32[2,128,128]{2,1,0:T(8,128)} %r_hbm.1, ...), custom_call_target="tpu_custom_call" | custom-call | tf_op jit(solution)/shard_map/exchange/pallas_call | solution.py:383
  206.8 3.4 %copy.10 = f32[256,8192]{1,0:T(8,128)} copy(f32[256,8192]{1,0:T(8,128)S(1)} %bitcast.3) | data formatting | bytes 16777216

commit v5 on v4

--- a/solution.py
+++ b/solution.py
@@ -49,16 +49,16 @@
 LEFT, RIGHT, PARTNER, FAR = 0, 1, 2, 3
 SPANS = [512, 2560, 2048, 1536, 1024, 512]
 GROUPS = len(SPANS)
+CROSS = (3,)
 LINES = 48
 BLOCK = 512
-HEAD = SLOTS + 8
 
 
 def exchange_kernel(
-    owned, flags, dest_ref, thin_ref, piv_ref, strip_ref, r_hbm, big_hbm,
+    wanted, flags, dest_ref, thin_ref, piv_ref, strip_ref, r_hbm, big_hbm,
     g,
     lines, rows, thin, ext, ext_out, tile, tile_sum, tile_in, low, hi_ref, lo_ref, pick_ref, r_ref, big_ref,
-    tile_s, tile_r, low_s, low_r, row_s, row_r, ext_s, ext_r, ag_s, ag_r, core_r, ag_l, row_l, ext_l, in_l, big_l,
+    tile_s, tile_r, low_s, low_r, low_z, low_over_r, ext_y, ext_in, row_s, row_r, ext_s, ext_r, ag_s, ag_r, core_r, ag_l, row_l, ext_l, in_l, big_l,
 ):
     r, c = lax.axis_index("row"), lax.axis_index("col")
     x, h, core = r // 4, lax.rem(r // 2, 2), lax.rem(r, 2)
@@ -138,9 +138,16 @@
         arrived(j, RIGHT)
         pl.when(jnp.logical_not(odd))(lambda: onward(j, RIGHT, ag_r.at[j, FAR], peer(3, 0, 0)))
         across(j, RIGHT)
+        if j in CROSS:
+            pl.when(odd)(lambda: onward(j, RIGHT, ag_r.at[j, 5], peer(0, 1, 0)))
+            pl.when(jnp.logical_not(odd))(lambda: onward(j, LEFT, ag_r.at[j, 4], peer(0, 1, 0)))
         arrived(j, PARTNER)
-        onward(j, PARTNER, ag_r.at[j, 4], peer(1, 0, 0))
-        onward(j, PARTNER, ag_r.at[j, 5], peer(3, 0, 0))
+        if j in CROSS:
+            pl.when(odd)(lambda: onward(j, PARTNER, ag_r.at[j, 5], peer(3, 0, 0)))
+            pl.when(jnp.logical_not(odd))(lambda: onward(j, PARTNER, ag_r.at[j, 4], peer(1, 0, 0)))
+        else:
+            onward(j, PARTNER, ag_r.at[j, 4], peer(1, 0, 0))
+            onward(j, PARTNER, ag_r.at[j, 5], peer(3, 0, 0))
         across(j, PARTNER)
 
     def far(j):
@@ -176,15 +183,7 @@
             s = pl.ds(pl.multiple_of(start + i * BLOCK, BLOCK), BLOCK)
             first = start // TILE + i * (BLOCK // TILE)
             mask = jnp.concatenate([jnp.full((1, TILE), flag(first + t), F32) for t in range(BLOCK // TILE)], axis=1)
-            part = thin[:, s] * mask
-            rows[:, :, s] = picked(part)
-            for t in range(BLOCK // TILE):
-                for k in range(2):
-                    chosen = jnp.where(owned[k] == first + t, 1.0, 0.0)
-                    into = pl.ds(0, TILE), pl.ds(k * TILE, TILE)
-                    tile[into] += part[:, t * TILE : (t + 1) * TILE] * chosen
-                at = pl.multiple_of(start + i * BLOCK + t * TILE, TILE)
-                tile[pl.ds(TILE, 8), pl.ds(0, TILE)] += piv_ref[pl.ds(0, 8), pl.ds(at, TILE)] * chosen
+            rows[:, :, s] = picked(thin[:, s] * mask)
             return 0
 
         lax.fori_loop(0, SPANS[j] // BLOCK, block, 0)
@@ -196,29 +195,61 @@
             send(rows.at[to, :, s], g.at[r, :, s], row_s.at[j], row_r.at[j], to).start()
         pltpu.make_async_copy(rows.at[r, :, s], g.at[r, :, s], row_l.at[j]).start()
 
+    def tile_along(k):
+        there = lax.rem(y + k, 4)
+        return send(tile.at[lax.rem(there, 2)], tile_in.at[k], tile_s.at[k], tile_r.at[k], r, along_y(k))
+
     def tile_across():
-        return send(tile, tile_in.at[0], tile_s.at[0], tile_r.at[0], r, across_z)
-
-    def tile_along(k):
-        return send(tile_sum, tile_in.at[k], tile_s.at[k], tile_r.at[k], r, along_y(k))
-
-    def tile_next():
-        tile_across().wait_recv()
-        tile_sum[...] = tile[...] + tile_in[0]
+        return send(tile_sum, tile_in.at[0], tile_s.at[0], tile_r.at[0], r, across_z)
+
+    def select():
+        def one(t, found):
+            s = pl.ds(pl.multiple_of(t * TILE, TILE), TILE)
+            part, head = thin[:, s], piv_ref[pl.ds(0, 8), s]
+            at = [jnp.where(wanted[k] == c * flags.shape[1] + t, 1.0, 0.0) for k in range(2)]
+            return (
+                found[0] + part * (flag(t) * at[0]),
+                found[1] + part * (flag(t) * at[1]),
+                found[2] + head * at[1],
+            )
+
+        none = jnp.zeros((TILE, TILE), F32)
+        found = lax.fori_loop(0, flags.shape[1], one, (none, none, jnp.zeros((8, TILE), F32)))
+        for k in range(2):
+            tile[k, pl.ds(0, TILE), :] = found[k]
+            tile[k, pl.ds(TILE, 8), :] = found[2]
+
+    def tile_begin():
         for k in (1, 2, 3):
             tile_along(k).start()
 
-    def ext_begin():
-        total = tile_sum[...]
+    def tile_next():
+        total = jnp.where(lax.rem(y, 2) == 0, tile[0], tile[1])
         for k in (1, 2, 3):
             tile_along(k).wait_recv()
             total = total + tile_in[k]
-        ext_out[:, pl.ds(0, SLOTS), :] = picked(total[:TILE, :])
-        ext_out[:, pl.ds(SLOTS, 8), :] = jnp.broadcast_to(total[TILE:, :][None], (16, 8, 2 * TILE))
+        tile_sum[...] = total
+        tile_across().start()
+
+    def ext_begin():
+        tile_across().wait_recv()
+        total = tile_sum[...] + tile_in[0]
+        slots = picked(total[:TILE, :])
+        ext_out[:, pl.ds(0, 8), :] = jnp.where(y < 2, slots[:, :8], slots[:, 8:])
+        ext_out[:, pl.ds(8, 8), :] = jnp.broadcast_to(total[TILE:, :][None], (16, 8, TILE))
         for off in OTHERS:
             to = peer(*off)
-            send(ext_out.at[to], ext.at[r], ext_s, ext_r, to).start()
-        pltpu.make_async_copy(ext_out.at[r], ext.at[r], ext_l).start()
+            send(ext_out.at[to], ext.at[y, r], ext_s, ext_r, to).start()
+        pltpu.make_async_copy(ext_out.at[r], ext.at[y, r], ext_l).start()
+
+    def ext_along(k):
+        return send(ext.at[y], ext.at[y], ext_y, ext_in, r, along_y(k))
+
+    def ext_next():
+        took(ext.at[y, pl.ds(0, 15)], ext_r)
+        took(ext.at[y, 0], ext_l)
+        for k in (1, 2, 3):
+            ext_along(k).start()
 
     def keep(parts, at):
         for ref, part in zip((hi_ref, lo_ref), parts):
@@ -230,24 +261,29 @@
     zero = jnp.zeros((16 * SLOTS, 1), F32)
 
     def factors():
-        took(ext.at[pl.ds(0, 15)], ext_r)
-        took(ext.at[0], ext_l)
+        took(ext.at[pl.ds(0, 3)], ext_in)
         for copy in constants:
             copy.wait()
-        terms = ext[:, :SLOTS, :].reshape(16 * SLOTS, 2 * TILE)
-        pivot = limbs(centred(ext[:, SLOTS:, :TILE].reshape(TILE, TILE)))
-        first = limbs(-subtract_product(zero, limbs(centred(terms[:, :TILE])), limbs(centred(r_ref[0]))))
-        second = subtract_product(terms[:, TILE:], first, pivot)
+        halves = [ext[k, :, :8, :] for k in range(4)]
+        terms = [jnp.concatenate([halves[k], halves[k + 2]], axis=1).reshape(16 * SLOTS, TILE) for k in range(2)]
+        pivot = limbs(centred(ext[0, :, 8:, :].reshape(TILE, TILE)))
+        first = limbs(-subtract_product(zero, limbs(centred(terms[0])), limbs(centred(r_ref[0]))))
+        second = subtract_product(terms[1], first, pivot)
         second = limbs(-subtract_product(zero, limbs(second), limbs(centred(r_ref[1]))))
         keep(first, 0)
         keep(second, TILE)
 
+    def quarter(k):
+        return low.at[pl.ds(k * (4 * SLOTS), 4 * SLOTS)]
+
     def low_out(k):
-        col = (1, 2, 3, 4)[k]
-        return send(low, low, low_s.at[k], low_r, r, col)
-
-    def low_next(k):
-        return send(low, low, low_s.at[k], low_r, r, 5 + k)
+        return send(low, low, low_s.at[k - 1], low_r, r, k)
+
+    def low_over():
+        return send(quarter(y), quarter(y), low_z, low_over_r, r, across_z)
+
+    def low_along(k):
+        return send(quarter(y), quarter(y), low_s.at[k - 1], low_r, r, along_y(k))
 
     def lower_begin():
         @pl.when(c == 0)
@@ -257,19 +293,28 @@
                 part = lines[:, 8 * k : 8 * k + 8, :PANEL].reshape(TILE, PANEL)
                 base = subtract_product(base, kept(k * TILE), limbs(centred(part)))
             low[...] = -subtract_product(zero, limbs(base), limbs(centred(big_ref[...])))
-            for k in (3, 0, 1, 2):
+            for k in (1, 3, 2):
                 low_out(k).start()
 
-        @pl.when(c == 4)
+    def lower_next():
+        @pl.when((plane == 0) & (y != 0))
         def _():
-            low_out(3).wait_recv()
-            for k in range(3):
-                low_next(k).start()
+            low_out(1).wait_recv()
+
+        @pl.when(plane == 0)
+        def _():
+            low_over().start()
+
+        @pl.when(plane == 1)
+        def _():
+            low_over().wait_recv()
+            for k in (1, 3, 2):
+                low_along(k).start()
 
     def lower_end():
-        @pl.when((c != 0) & (c != 4))
+        @pl.when(plane == 1)
         def _():
-            low_out(3).wait_recv()
+            took(low.at[pl.ds(0, 12 * SLOTS)], low_r)
 
         keep(limbs(low[...]), 2 * TILE)
 
@@ -301,57 +346,59 @@
     own(0)
     own(1)
     choose()
-    tile[...] = jnp.zeros_like(tile)
     for j in range(GROUPS):
         thin_in(j).wait()
+    select()
+    tile_begin()
     fill(0)
     rows_out(0)
     near(0)
+    tile_next()
+    far(0)
+    ext_begin()
+    own(2)
     fill(1)
+    rows_out(1)
+    last(0)
+    ext_next()
+    own(3)
     fill(2)
-    far(0)
-    fill(3)
-    fill(4)
-    fill(5)
-    tile_across().start()
-    last(0)
-    own(2)
-    own(3)
     near(1)
-    tile_next()
-    own(4)
-    own(5)
-    ext_begin()
-    near(2)
-    rows_out(1)
-    far(1)
-    near(3)
     factors()
     complete(0)
     lower_begin()
+    rows_out(2)
+    own(4)
+    fill(3)
+    near(2)
+    far(1)
+    lower_next()
+    own(5)
+    rows_out(3)
+    fill(4)
+    fill(5)
+    near(3)
+    far(2)
+    last(1)
+    lower_end()
+    rows_out(4)
     near(4)
-    near(5)
-    far(2)
-    rows_out(2)
-    last(1)
+    compute(0)
     far(3)
     last(2)
-    rows_out(3)
-    far(4)
-    far(5)
-    rows_out(4)
     rows_out(5)
-    lower_end()
-    compute(0)
-    last(3)
+    near(5)
     complete(1)
     compute(1)
-    last(4)
+    far(4)
+    last(3)
     complete(2)
     compute(2)
-    last(5)
+    far(5)
+    last(4)
     complete(3)
     compute(3)
+    last(5)
     complete(4)
     compute(4)
     complete(5)
@@ -360,26 +407,31 @@
     for j in range(GROUPS):
         took(lines.at[pl.ds(0, 15), :, columns(j)], ag_s.at[j])
         took(g.at[pl.ds(0, 15), :, columns(j)], row_s.at[j])
-    took(ext.at[pl.ds(0, 15)], ext_s)
+    took(ext.at[0, pl.ds(0, 15)], ext_s)
+    took(ext.at[pl.ds(0, 3)], ext_y)
     tile_across().wait_send()
     for k in (1, 2, 3):
         tile_along(k).wait_send()
 
     @pl.when(c == 0)
     def _():
-        for k in range(4):
+        for k in (1, 2, 3):
             low_out(k).wait_send()
 
-    @pl.when(c == 4)
+    @pl.when(plane == 0)
     def _():
-        for k in range(3):
-            low_next(k).wait_send()
-
-
-def exchange(owned, flags, dest, thin, piv, strip, recips, big):
+        low_over().wait_send()
+
+    @pl.when(plane == 1)
+    def _():
+        for k in (1, 2, 3):
+            low_along(k).wait_send()
+
+
+def exchange(wanted, flags, dest, thin, piv, strip, recips, big):
     width = thin.shape[1]
     dma = pltpu.SemaphoreType.DMA
-    head = (TILE + 8, 2 * TILE)
+    head = (TILE + 8, TILE)
     return pl.pallas_call(
         exchange_kernel,
         in_specs=[SM, SM, VM, ANY, VM, ANY, ANY, ANY],
@@ -389,9 +441,9 @@
             pltpu.VMEM((16, LINES, width), F32),
             pltpu.VMEM((16, SLOTS, width), F32),
             pltpu.VMEM(thin.shape, F32),
-            pltpu.VMEM((16, HEAD, 2 * TILE), F32),
-            pltpu.VMEM((16, HEAD, 2 * TILE), F32),
-            pltpu.VMEM(head, F32),
+            pltpu.VMEM((4, 16, SLOTS, TILE), F32),
+            pltpu.VMEM((16, SLOTS, TILE), F32),
+            pltpu.VMEM((2,) + head, F32),
             pltpu.VMEM(head, F32),
             pltpu.VMEM((4,) + head, F32),
             pltpu.VMEM((16 * SLOTS, PANEL), F32),
@@ -400,7 +452,7 @@
             pltpu.VMEM((16 * SLOTS, TILE), BF16),
             pltpu.VMEM(recips.shape, F32),
             pltpu.VMEM(big.shape, F32),
-            dma((4,)), dma((4,)), dma((4,)), dma(()),
+            dma((4,)), dma((4,)), dma((3,)), dma(()), dma(()), dma(()), dma(()), dma(()),
             dma((GROUPS,)), dma((GROUPS,)), dma(()), dma(()),
             dma((GROUPS,)), dma((GROUPS, 7)), dma((GROUPS,)),
             dma((GROUPS,)), dma((GROUPS,)), dma(()), dma((GROUPS,)), dma((2,)),
@@ -409,13 +461,12 @@
         compiler_params=pltpu.CompilerParams(
             collective_id=0, has_side_effects=True, vmem_limit_bytes=52 << 20
         ),
-    )(owned, flags, dest, thin, piv, strip, recips, big)
+    )(wanted, flags, dest, thin, piv, strip, recips, big)
 
 
 def local(thin, flags, tiles, pivots, recips, dest, strip, big):
     width = thin.shape[1]
-    owned = tiles - lax.axis_index("col") * (width // TILE)
-    out = exchange(owned, flags, dest[None, :], thin, pivots.reshape(16, width), strip, recips, big)
+    out = exchange(tiles, flags, dest[None, :], thin, pivots.reshape(16, width), strip, recips, big)
     return out.reshape(16 * SLOTS, width)
 
 

time: 211 us -> 195 us (0.924)
  Pallas kernels: 206 us -> 191 us
    pallas_call x1, Pallas kernels: 206 us -> 191 us  [exchange(): pl.pallas_call(exchange_kernel, in_specs=[SM, SM, VM, ANY, VM, ANY, ANY,...]
where the time goes in v5:
time: 195 us; the launch traced here: 194 us
  Pallas kernels  191 us (98%)
  local copies, waits for them, and re-layouts  3.4 us (2%)
    pallas_call x1, Pallas kernels, exchange(): pl.pallas_call(exchange_kernel, in_specs=[SM, SM, VM, ANY, VM, ANY, ANY,...  191 us

profile of v5, /device:TPU:1, one launch (start us, length us, event | category | flops | bytes accessed | tf_op | source)
XLA Modules:
  0.0 194.3 jit_solution(3698036942363034166)
XLA Ops:
  0.0 190.9 %exchange.1 = f32[16,16,8192]{2,1,0:T(8,128)S(1)} custom-call(s32[2]{0:T(128)} %wanted.1, s32[1,64]{1,0:T(1,128)} %flags.1, s32[1,128]{1,0:T(1,128)} %bitcast.5, f32[128,8192]{1,0:T(8,128)} %thin_ref.1, f32[16,8192]{1,0:T(8,128)} %bitcast.4, f32[32,8192]{1,0:T(8,128)} %strip_ref.1, f32[2,128,128]{2,1,0:T(8,128)} %r_hbm.1, f32[512,512]{1,0:T(8,128)} %big_hbm.1), custom_call_target="tpu_custom_call" | custom-call | tf_op jit(solution)/shard_map/exchange/pallas_call | solution.py:435
  190.9 3.4 %copy.10 = f32[256,8192]{1,0:T(8,128)} copy(f32[256,8192]{1,0:T(8,128)S(1)} %bitcast.3) | data formatting | bytes 16777216

commit v6 on v5

--- a/solution.py
+++ b/solution.py
@@ -36,11 +36,15 @@
     return high.astype(BF16), (values - high * 256.0).astype(BF16)
 
 
-def subtract_product(base, left, right):
+def product(left, right):
     (a_hi, a_lo), (b_hi, b_lo) = left, right
     cross = nearest(nearest(dot(a_hi, b_lo)) + dot(a_lo, b_hi))
     upper = nearest(256.0 * cross + 15.0 * nearest(dot(a_hi, b_hi)))
-    return nearest(base - upper - dot(a_lo, b_lo))
+    return upper + dot(a_lo, b_lo)
+
+
+def subtract_product(base, left, right):
+    return nearest(base - product(left, right))
 
 
 OTHERS = [(1, 1, 0), (3, 0, 0), (3, 1, 0), (1, 0, 0), (2, 1, 0), (2, 0, 0), (0, 1, 0),
@@ -50,6 +54,7 @@
 SPANS = [512, 2560, 2048, 1536, 1024, 512]
 GROUPS = len(SPANS)
 CROSS = (3,)
+LATE = 3
 LINES = 48
 BLOCK = 512
 
@@ -57,7 +62,7 @@
 def exchange_kernel(
     wanted, flags, dest_ref, thin_ref, piv_ref, strip_ref, r_hbm, big_hbm,
     g,
-    lines, rows, thin, ext, ext_out, tile, tile_sum, tile_in, low, hi_ref, lo_ref, pick_ref, r_ref, big_ref,
+    lines, rows, thin, ready, ext, ext_out, tile, tile_sum, tile_in, low, hi_ref, lo_ref, pick_ref, r_ref, big_ref,
     tile_s, tile_r, low_s, low_r, low_z, low_over_r, ext_y, ext_in, row_s, row_r, ext_s, ext_r, ag_s, ag_r, core_r, ag_l, row_l, ext_l, in_l, big_l,
 ):
     r, c = lax.axis_index("row"), lax.axis_index("col")
@@ -318,30 +323,47 @@
 
         keep(limbs(low[...]), 2 * TILE)
 
-    def complete(j):
-        s = columns(j)
-        took(lines.at[pl.ds(0, 8), :, s], core_r.at[j])
+    def lines_done(j):
+        took(lines.at[pl.ds(0, 8), :, columns(j)], core_r.at[j])
         took(slab(j, r), ag_l.at[j])
-        took(g.at[pl.ds(0, 15), :, s], row_r.at[j])
-        took(g.at[0, :, s], row_l.at[j])
-
-    def compute(j):
-        start = sum(SPANS[:j])
-
+
+    def rows_done(j):
+        took(g.at[pl.ds(0, 15), :, columns(j)], row_r.at[j])
+        took(g.at[0, :, columns(j)], row_l.at[j])
+
+    def each_block(j, body):
         def block(i, _):
-            s = pl.ds(pl.multiple_of(start + i * BLOCK, BLOCK), BLOCK)
+            body(pl.multiple_of(sum(SPANS[:j]) + i * BLOCK, BLOCK))
+            return 0
+
+        lax.fori_loop(0, SPANS[j] // BLOCK, block, 0)
+
+    def ready_at(at):
+        return pl.ds(pl.multiple_of(at - sum(SPANS[:LATE]), BLOCK), BLOCK)
+
+    def put(s, amount):
+        result = nearest(g[:, :, s].reshape(16 * SLOTS, BLOCK) - amount)
+        result = jnp.where(result < 0.0, result + MODULUS, result) * INVERSE
+        g[:, :, s] = result.reshape(16, SLOTS, BLOCK)
+
+    def compute(j, early=False):
+        def body(at):
+            s = pl.ds(at, BLOCK)
             held = lines[:, :, s]
             inner = jnp.concatenate(
                 [held[:, 0:8].reshape(TILE, BLOCK), held[:, 8:16].reshape(TILE, BLOCK),
                  held[:, 16:].reshape(PANEL, BLOCK)], axis=0
             )
-            base = g[:, :, s].reshape(16 * SLOTS, BLOCK)
-            result = subtract_product(base, (hi_ref[...], lo_ref[...]), limbs(centred(inner)))
-            result = jnp.where(result < 0.0, result + MODULUS, result) * INVERSE
-            g[:, :, s] = result.reshape(16, SLOTS, BLOCK)
-            return 0
-
-        lax.fori_loop(0, SPANS[j] // BLOCK, block, 0)
+            amount = product((hi_ref[...], lo_ref[...]), limbs(centred(inner)))
+            if early:
+                ready[:, ready_at(at)] = amount
+            else:
+                put(s, amount)
+
+        each_block(j, body)
+
+    def finish(j):
+        each_block(j, lambda at: put(pl.ds(at, BLOCK), ready[:, ready_at(at)]))
 
     own(0)
     own(1)
@@ -365,7 +387,8 @@
     fill(2)
     near(1)
     factors()
-    complete(0)
+    lines_done(0)
+    rows_done(0)
     lower_begin()
     rows_out(2)
     own(4)
@@ -374,35 +397,43 @@
     far(1)
     lower_next()
     own(5)
-    rows_out(3)
     fill(4)
     fill(5)
     near(3)
+    rows_out(3)
     far(2)
     last(1)
     lower_end()
+    near(4)
     rows_out(4)
-    near(4)
     compute(0)
     far(3)
     last(2)
+    near(5)
     rows_out(5)
-    near(5)
-    complete(1)
+    lines_done(1)
+    rows_done(1)
     compute(1)
     far(4)
     last(3)
-    complete(2)
+    lines_done(2)
+    rows_done(2)
     compute(2)
     far(5)
     last(4)
-    complete(3)
-    compute(3)
+    lines_done(3)
+    compute(3, early=True)
+    lines_done(4)
+    compute(4, early=True)
     last(5)
-    complete(4)
-    compute(4)
-    complete(5)
-    compute(5)
+    lines_done(5)
+    compute(5, early=True)
+    rows_done(3)
+    finish(3)
+    rows_done(4)
+    finish(4)
+    rows_done(5)
+    finish(5)
 
     for j in range(GROUPS):
         took(lines.at[pl.ds(0, 15), :, columns(j)], ag_s.at[j])
@@ -441,6 +472,7 @@
             pltpu.VMEM((16, LINES, width), F32),
             pltpu.VMEM((16, SLOTS, width), F32),
             pltpu.VMEM(thin.shape, F32),
+            pltpu.VMEM((16 * SLOTS, sum(SPANS[LATE:])), F32),
             pltpu.VMEM((4, 16, SLOTS, TILE), F32),
             pltpu.VMEM((16, SLOTS, TILE), F32),
             pltpu.VMEM((2,) + head, F32),

time: 195 us -> 192 us (0.985)
  Pallas kernels: 191 us -> 188 us
    pallas_call x1, Pallas kernels: 191 us -> 188 us  [exchange(): pl.pallas_call(exchange_kernel, in_specs=[SM, SM, VM, ANY, VM, ANY, ANY,...]
where the time goes in v6:
time: 192 us
  Pallas kernels  188 us (98%)
  local copies, waits for them, and re-layouts  3.4 us (2%)
    pallas_call x1, Pallas kernels, exchange(): pl.pallas_call(exchange_kernel, in_specs=[SM, SM, VM, ANY, VM, ANY, ANY,...  188 us

profile of v6, /device:TPU:1, one launch (start us, length us, event | category | flops | bytes accessed | tf_op | source)
XLA Modules:
  0.0 191.9 jit_solution(1403401668652585089)
XLA Ops:
  0.0 188.5 %exchange.1 = f32[16,16,8192]{2,1,0:T(8,128)S(1)} custom-call(s32[2]{0:T(128)} %wanted.1, s32[1,64]{1,0:T(1,128)} %flags.1, s32[1,128]{1,0:T(1,128)} %bitcast.5, f32[128,8192]{1,0:T(8,128)} %thin_ref.1, f32[16,8192]{1,0:T(8,128)} %bitcast.4, f32[32,8192]{1,0:T(8,128)} %strip_ref.1, f32[2,128,128]{2,1,0:T(8,128)} %r_hbm.1, f32[512,512]{1,0:T(8,128)} %big_hbm.1), custom_call_target="tpu_custom_call" | custom-call | tf_op jit(solution)/shard_map/exchange/pallas_call | solution.py:466
  188.5 3.4 %copy.10 = f32[256,8192]{1,0:T(8,128)} copy(f32[256,8192]{1,0:T(8,128)S(1)} %bitcast.3) | data formatting | bytes 16777216

commit v7 on v6

--- a/solution.py
+++ b/solution.py
@@ -59,10 +59,50 @@
 BLOCK = 512
 
 
+def residue(moved, amount):
+    result = nearest(moved.reshape(amount.shape) - amount)
+    return (jnp.where(result < 0.0, result + MODULUS, result) * INVERSE).reshape(moved.shape)
+
+
+def close_kernel(g, ready, out_ref, done, sems):
+    copies = []
+
+    def leave(src, s):
+        copies.append(pltpu.make_async_copy(src, out_ref.at[:, :, s], sems.at[len(copies)]))
+        copies[-1].start()
+
+    early = sum(SPANS[:LATE])
+    for j in range(LATE):
+        s = pl.ds(sum(SPANS[:j]), SPANS[j])
+        leave(g.at[:, :, s], s)
+    for at in range(0, sum(SPANS[LATE:]), BLOCK):
+        s = pl.ds(early + at, BLOCK)
+        done[:, :, pl.ds(at, BLOCK)] = residue(g[:, :, s], ready[:, pl.ds(at, BLOCK)])
+        leave(done.at[:, :, pl.ds(at, BLOCK)], s)
+    for copy in copies:
+        copy.wait()
+
+
+def close(g, ready):
+    late = ready.shape[1]
+    return pl.pallas_call(
+        close_kernel,
+        in_specs=[VM, VM],
+        out_specs=ANY,
+        out_shape=jax.ShapeDtypeStruct(g.shape, F32),
+        scratch_shapes=[
+            pltpu.VMEM((16, SLOTS, late), F32),
+            pltpu.SemaphoreType.DMA((LATE + late // BLOCK,)),
+        ],
+        name="close",
+        compiler_params=pltpu.CompilerParams(vmem_limit_bytes=16 << 20),
+    )(g, ready)
+
+
 def exchange_kernel(
     wanted, flags, dest_ref, thin_ref, piv_ref, strip_ref, r_hbm, big_hbm,
-    g,
-    lines, rows, thin, ready, ext, ext_out, tile, tile_sum, tile_in, low, hi_ref, lo_ref, pick_ref, r_ref, big_ref,
+    g, ready,
+    lines, rows, thin, ext, ext_out, tile, tile_sum, tile_in, low, hi_ref, lo_ref, pick_ref, r_ref, big_ref,
     tile_s, tile_r, low_s, low_r, low_z, low_over_r, ext_y, ext_in, row_s, row_r, ext_s, ext_r, ag_s, ag_r, core_r, ag_l, row_l, ext_l, in_l, big_l,
 ):
     r, c = lax.axis_index("row"), lax.axis_index("col")
@@ -342,9 +382,7 @@
         return pl.ds(pl.multiple_of(at - sum(SPANS[:LATE]), BLOCK), BLOCK)
 
     def put(s, amount):
-        result = nearest(g[:, :, s].reshape(16 * SLOTS, BLOCK) - amount)
-        result = jnp.where(result < 0.0, result + MODULUS, result) * INVERSE
-        g[:, :, s] = result.reshape(16, SLOTS, BLOCK)
+        g[:, :, s] = residue(g[:, :, s], amount)
 
     def compute(j, early=False):
         def body(at):
@@ -361,9 +399,6 @@
                 put(s, amount)
 
         each_block(j, body)
-
-    def finish(j):
-        each_block(j, lambda at: put(pl.ds(at, BLOCK), ready[:, ready_at(at)]))
 
     own(0)
     own(1)
@@ -429,11 +464,8 @@
     lines_done(5)
     compute(5, early=True)
     rows_done(3)
-    finish(3)
     rows_done(4)
-    finish(4)
     rows_done(5)
-    finish(5)
 
     for j in range(GROUPS):
         took(lines.at[pl.ds(0, 15), :, columns(j)], ag_s.at[j])
@@ -466,13 +498,15 @@
     return pl.pallas_call(
         exchange_kernel,
         in_specs=[SM, SM, VM, ANY, VM, ANY, ANY, ANY],
-        out_specs=VM,
-        out_shape=pltpu.VMEM((16, SLOTS, width), F32),
+        out_specs=[VM, VM],
+        out_shape=[
+            pltpu.VMEM((16, SLOTS, width), F32),
+            pltpu.VMEM((16 * SLOTS, sum(SPANS[LATE:])), F32),
+        ],
         scratch_shapes=[
             pltpu.VMEM((16, LINES, width), F32),
             pltpu.VMEM((16, SLOTS, width), F32),
             pltpu.VMEM(thin.shape, F32),
-            pltpu.VMEM((16 * SLOTS, sum(SPANS[LATE:])), F32),
             pltpu.VMEM((4, 16, SLOTS, TILE), F32),
             pltpu.VMEM((16, SLOTS, TILE), F32),
             pltpu.VMEM((2,) + head, F32),
@@ -491,15 +525,15 @@
         ],
         name="exchange",
         compiler_params=pltpu.CompilerParams(
-            collective_id=0, has_side_effects=True, vmem_limit_bytes=52 << 20
+            collective_id=0, has_side_effects=True, vmem_limit_bytes=48 << 20
         ),
     )(wanted, flags, dest, thin, piv, strip, recips, big)
 
 
 def local(thin, flags, tiles, pivots, recips, dest, strip, big):
     width = thin.shape[1]
-    out = exchange(tiles, flags, dest[None, :], thin, pivots.reshape(16, width), strip, recips, big)
-    return out.reshape(16 * SLOTS, width)
+    g, ready = exchange(tiles, flags, dest[None, :], thin, pivots.reshape(16, width), strip, recips, big)
+    return close(g, ready).reshape(16 * SLOTS, width)
 
 
 def solution(mesh):

time: 192 us -> 191 us (level)
  local copies, waits for them, and re-layouts: 3.4 us -> 0 us
  Pallas kernels: 188 us -> 191 us
    unnamed x1 -> x0, local copies, waits for them, and re-layouts: 3.4 us -> none
    pallas_call x0 -> x1, Pallas kernels: none -> 3.39 us  [close(): pl.pallas_call(close_kernel, in_specs=[VM, VM], out_specs=ANY, out_shape=...]
where the time goes in v7:
time: 191 us
  Pallas kernels  191 us (100%)
    pallas_call x1, Pallas kernels, exchange(): pl.pallas_call(exchange_kernel, in_specs=[SM, SM, VM, ANY, VM, ANY, ANY,...  187 us

profile of v7, /device:TPU:1, one launch (start us, length us, event | category | flops | bytes accessed | tf_op | source)
XLA Modules:
  0.0 191.0 jit_solution(12324807705779094730)
XLA Ops:
  0.0 187.5 %exchange.1 = (f32[16,16,8192]{2,1,0:T(8,128)S(1)}, f32[256,3072]{1,0:T(8,128)S(1)}) custom-call(s32[2]{0:T(128)} %wanted.1, s32[1,64]{1,0:T(1,128)} %flags.1, s32[1,128]{1,0:T(1,128)} %bitcast.4, f32[128,8192]{1,0:T(8,128)} %thin_ref.1, f32[16,8192]{1,0:T(8,128)} %bitcast.3, f32[32,8192]{1,0:T(8,128)} %strip_ref.1, f32[2,128,128]{2,1,0:T(8,128)} %r_hbm.1, ...), custom_call_target="tpu_custom_call" | custom-call | tf_op jit(solution)/shard_map/exchange/pallas_call | solution.py:498
  187.5 3.4 %close.1 = f32[16,16,8192]{2,1,0:T(8,128)} custom-call(f32[16,16,8192]{2,1,0:T(8,128)S(1)} %get-tuple-element.7.g, f32[256,3072]{1,0:T(8,128)S(1)} %get-tuple-element.8.ready), custom_call_target="tpu_custom_call" | custom-call | tf_op jit(solution)/shard_map/close/pallas_call | solution.py:88
